TPU v7x, 32 devices: a whole 2x2x4 slice. The times are simulated.
32 devices in a mesh: epoch: 4 (over z), vel: 8 (over y, x, core).
Axes of the slice: x: 2, y: 2, z: 4, core: 2. Of those that a mesh axis runs over, the one named last changes fastest.
Arguments:
- science: float32 [8, 32, 1024], P('epoch', 'vel'), may hold values from -6 to 6
- variance: float32 [8, 32, 1024], P('epoch', 'vel'), may hold values from 0.25 to 4
- psf: float32 [8, 9], P('epoch'), may hold values from 0.05 to 1
- shifts: int32 [2, 8, 8], P(None, None, 'vel'), may hold values from -16 to 16, as said below
Outputs:
- likelihood: float32 [8, 32, 1024], P('vel', 'epoch')
Inputs may be any that keep to these rules, and one draw needn't show every extreme that they name: For each velocity, the shifts of epoch e are the floor of the velocity's integer rates times the epoch's time over the span of the times; the first epoch's shifts are zero, and times rise with the epoch.
All inputs are finite; a program needn't handle non-finite values.
Results may differ from a plain program's by a relative error of at most 0.0003.
Values sent between devices are 32-bit elements; how exact they have to be, the bound alone decides.
No kernel may reach another device: no remote copies, remote signals or barrier semaphores. Data moves between devices by JAX's collectives and lax.ppermute only.
A program may use at most 64 MiB of HBM per device.

v0:
```python
import jax
import jax.numpy as jnp
from jax import lax
from jax.sharding import PartitionSpec as P

MAXS = 16


def extended(block, sides, width):
    for axis, dim in sides:
        count = lax.axis_size(axis)
        forward = [(i, i + 1) for i in range(count - 1)]
        backward = [(target, source) for source, target in forward]
        low = lax.ppermute(
            lax.slice_in_dim(block, block.shape[dim] - width, None, axis=dim), axis, forward
        )
        high = lax.ppermute(lax.slice_in_dim(block, 0, width, axis=dim), axis, backward)
        block = jnp.concatenate([low, block, high], axis=dim)
    return block


def filter_columns(pairing, weights):
    radius = weights.shape[2] // 2
    breadth = pairing.shape[3]
    padded = jnp.pad(pairing, ((0, 0), (0, 0), (0, 0), (radius, radius)))
    summed = jnp.zeros_like(pairing)
    for offset in range(weights.shape[2]):
        summed = (
            summed + weights[:, :, offset, None, None] * padded[:, :, :, offset : offset + breadth]
        )
    return summed


def filter_rows(rimmed, weights, height):
    summed = jnp.zeros(rimmed.shape[:2] + (height, rimmed.shape[3]), jnp.float32)
    for offset in range(weights.shape[2]):
        summed = (
            summed + weights[:, :, offset, None, None] * rimmed[:, :, offset : offset + height, :]
        )
    return summed


def per_device(science, variance, psf, shifts):
    slots = science.shape[0]
    height = science.shape[1]
    breadth = science.shape[2]
    radius = psf.shape[1] // 2
    pairing = jnp.stack([science / variance, 1.0 / variance], axis=1)
    weights = jnp.stack([psf, psf * psf], axis=1)
    columns_pass = filter_columns(pairing, weights)
    rimmed = extended(columns_pass, (("vel", 2),), radius)
    filtered = filter_rows(rimmed, weights, height)
    local_shifts = lax.dynamic_slice_in_dim(shifts, lax.axis_index("epoch") * slots, slots, 1)
    velocities = shifts.shape[2]
    gathered = lax.all_gather(filtered, "vel", axis=2, tiled=True)
    rows_all = gathered.shape[2]
    padded = jnp.pad(gathered, ((0, 0), (0, 0), (MAXS, MAXS), (MAXS, MAXS)))
    stacks = jnp.zeros((velocities, 2, rows_all, breadth), jnp.float32)
    for epoch_slot in range(slots):
        image = padded[epoch_slot]

        def window_at(shift_col, shift_row):
            return lax.dynamic_slice(
                image, (jnp.int32(0), MAXS + shift_row, MAXS + shift_col), (2, rows_all, breadth)
            )

        stacks = stacks + jax.vmap(window_at)(
            local_shifts[0, epoch_slot], local_shifts[1, epoch_slot]
        )
    mine = lax.psum_scatter(stacks, "epoch", scatter_dimension=2, tiled=True)
    return mine[:, 0] / jnp.sqrt(mine[:, 1])


def solution(mesh):
    return jax.shard_map(
        per_device,
        mesh=mesh,
        in_specs=(
            P("epoch", "vel", None),
            P("epoch", "vel", None),
            P("epoch", None),
            P(None, None, "vel"),
        ),
        out_specs=P("vel", "epoch", None),
        check_vma=False,
    )
```

profile of v0, /device:TPU:0, one launch (start us, length us, event | category | flops | bytes accessed | tf_op | source)
XLA Modules:
  0.0 81.5 jit_solution(1506419152563569825)
XLA Ops:
  6.5 0.0 all-reduce.5.cloned.1.call-start
  6.5 0.7 multiply_bitcast_fusion
  7.2 1.1 %fusion.26 = (f32[2,2,1]{2,0,1:T(2,128)S(1)}, f32[2,2,1]{2,0,1:T(2,128)S(1)}, f32[2,2,1]{2,0,1:T(2,128)S(1)}, f32[2,2,1]{2,0,1:T(2,128)S(1)}, f32[2,2,1]{2,0,1:T...) fusion(f32[2,1,9]{2,0,1:T(2,128)} %bitcast.58, ...), kind=kLoop, calls=%fused_computation.63 | loop fusion | flops 36 | bytes 288 | tf_op jit(solution)/shard_map/stack | solution.py:49
  8.3 0.1 copy.63
  8.4 0.1 copy.64
  8.5 0.1 copy.65
  8.6 0.1 copy.66
  8.7 0.1 copy.67
  8.8 0.1 copy.68
  8.9 0.1 copy.60
  9.0 0.1 copy.61
  9.1 0.1 copy.62
  9.2 0.8 divide_bitcast_fusion.1
  10.0 0.4 multiply_add_fusion
  10.4 2.4 %collective-permute-start = (f32[2,2,4,1024]{3,2,0,1:T(4,128)S(1)}, f32[2,2,4,1024]{3,2,0,1:T(4,128)S(1)}, u32[]{:S(2)}, u32[]{:S(2)}) collective-permute-start(f32[2,2,4,1024]{3,2,0,1:T(4,128)S(1)} %multiply_add_fusion), channel_id=1, source_target_pairs={{0,1},{1,2},{2,3},{3,4},{4,5},{5,6},{6,7},{8,9},{9,10},{10,11},{11... | collective-permute-start | bytes 196616 | tf_op jit(solution)/shard_map/ppermute | solution.py:14
  12.8 1.3 %collective-permute-start.1 = (f32[2,2,4,1024]{3,2,0,1:T(4,128)S(1)}, f32[2,2,4,1024]{3,2,0,1:T(4,128)S(1)}, u32[]{:S(2)}, u32[]{:S(2)}) collective-permute-start(f32[2,2,4,1024]{3,2,0,1:T(4,128)S(1)} %multiply_add_fusion), channel_id=1, source_target_pairs={{1,0},{2,1},{3,2},{4,3},{5,4},{6,5},{7,6},{9,8},{10,9},{11,10},{12... | collective-permute-start | bytes 196616 | tf_op jit(solution)/shard_map/ppermute | solution.py:17
  14.1 1.4 %constant_dynamic-slice_fusion = (s32[1,1,1]{1,2,0:T(1,128)}, s32[1,1,1]{1,2,0:T(1,128)}, s32[1,1,1]{1,2,0:T(1,128)}, s32[1,1,1]{1,2,0:T(1,128)}) fusion(s32[2,8,1]{1,2,0:T(1,128)} %param.7, s32[]{:T(128)S(6)} %select_n.15, s32[]{:T(128)S(6)} %add.166, s32[]{:T(128)S(6)} %add.168), kind=kLoop, calls=%fused_computation.71 | loop fusion | bytes 44 | tf_op jit(solution)/shard_map/slice | solution.py:68
  20.4 0.0 collective-permute-done
  20.5 0.0 collective-permute-done.1
  20.5 0.3 fusion.4
  20.7 0.1 copy.58
  20.8 14.1 %all_gather.3 = f32[2,2,32,1024]{3,1,0,2:T(2,128)S(1)} all-gather(f32[2,2,4,1024]{3,1,0,2:T(2,128)S(1)} %copy.58), channel_id=1, replica_groups=mesh['epoch'=4,'vel'=8] {'vel'}, dimensions={2}, use_global_device_ids=true | all-gather | bytes 589824 | tf_op jit(solution)/shard_map/all_gather | solution.py:55
  34.9 0.7 pad_slice_fusion.1
  35.6 0.0 copy-start
  35.7 1.3 %dynamic-slice_add_fusion = f32[1,2,32,1024]{3,1,0,2:T(2,128)} fusion(f32[1,2,64,1056]{3,1,0,2:T(2,128)S(1)} %get-tuple-element.28, s32[]{:T(128)} %bitcast.30, s32[]{:T(128)} %bitcast.33, f32[1,2,64,1056]{3,1,0,2:T(2,128)S(1)} %get-tuple-element.27, s32[]{:T(128)} %bitcast.24, s32[]{:T(128)} %bitcast.27), kind=kLoop, calls=%fused_computation.2 | loop fusion | flops 65536 | bytes 786448 | tf_op jit(solution)/shard_map/add | solution.py:67
  37.0 0.0 all-reduce.5.cloned.1.call-update
  37.0 0.0 copy-done
  37.0 0.6 dynamic-slice.10
  38.3 34.8 %all-reduce.5.cloned.1.call-done = f32[1,2,32,1024]{3,1,0,2:T(2,128)} async-done(((f32[1,2,32,1024]{3,1,0,2:T(2,128)}), f32[1,2,32,1024]{3,1,0,2:T(2,128)}) %all-reduce.5.cloned.1.call-update) | async-done | bytes 262160
  73.0 1.0 %fusion.24 = f32[1,8,1024]{2,0,1:T(1,128)S(1)} fusion(f32[1,2,32,1024]{3,1,0,2:T(2,128)} %all-reduce.5.cloned.1.call-done, u32[]{:T(128)S(6)} %convert, u32[]{:T(128)S(6)} %multiply.11), kind=kLoop, calls=%fused_computation.45 | loop fusion | flops 8192 | bytes 98312 | tf_op jit(solution)/shard_map/div | solution.py:71
  74.0 0.6 copy.59
  (1 shorter events, 0.0 us)
Async XLA Ops:
  6.5 66.5 %all-reduce.5.cloned.1.call-start = ((), (), s32[]{:S(2)}) async-start(), calls=%async_computation | async-start | bytes 524288
  10.4 10.0 %collective-permute-start = (f32[2,2,4,1024]{3,2,0,1:T(4,128)S(1)}, f32[2,2,4,1024]{3,2,0,1:T(4,128)S(1)}, u32[]{:S(2)}, u32[]{:S(2)}) collective-permute-start(f32[2,2,4,1024]{3,2,0,1:T(4,128)S(1)} %multiply_add_fusion), channel_id=1, source_target_pairs={{0,1},{1,2},{2,3},{3,4},{4,5},{5,6},{6,7},{8,9},{9,10},{10,11},{11... | collective-permute-start | bytes 196616 | tf_op jit(solution)/shard_map/ppermute | solution.py:14
  12.8 7.6 %collective-permute-start.1 = (f32[2,2,4,1024]{3,2,0,1:T(4,128)S(1)}, f32[2,2,4,1024]{3,2,0,1:T(4,128)S(1)}, u32[]{:S(2)}, u32[]{:S(2)}) collective-permute-start(f32[2,2,4,1024]{3,2,0,1:T(4,128)S(1)} %multiply_add_fusion), channel_id=1, source_target_pairs={{1,0},{2,1},{3,2},{4,3},{5,4},{6,5},{7,6},{9,8},{10,9},{11,10},{12... | collective-permute-start | bytes 196616 | tf_op jit(solution)/shard_map/ppermute | solution.py:17
  35.6 1.4 %copy-start = (u32[32]{0:T(128)S(1)}, u32[32]{0:T(128)}, u32[]{:S(2)}) copy-start(u32[32]{0:T(128)} %constant.89) | copy-start | bytes 388
Sparse Core Ops, SparseCore 0:
  37.1 35.8 all-reduce.4
where the time goes:
time: 81.9 us; the launch traced here: 81.5 us
  waiting for transfers between devices  34.8 us (42%)
  between operations  19.1 us (23%)
  blocking collectives  14.1 us (17%)
  other arithmetic  5.5 us (7%)
  local copies, waits for them, and re-layouts  4.27 us (5%)
  starting transfers between devices  3.69 us (5%)
    unnamed x2, waiting for transfers between devices  34.8 us
    all_gather x1, blocking collectives, per_device(): gathered = lax.all_gather(filtered, 'vel', axis=2, tiled=True)  14.1 us
    ppermute x1, starting transfers between devices, extended(): lax.ppermute(lax.slice_in_dim(block, block.shape[dim] - width, None, axis...  2.4 us
    another operation x2, other arithmetic, per_device(): weights = jnp.stack([psf, psf * psf], axis=1)  1.77 us
  transfers between devices with their start and end apart: 3, of which 1 were waited for; matrix products, arithmetic and copies ran while one was open for 2% of the time, Pallas kernels for 0%

commit v1 on v0

v1 whole, which is shorter than its diff:
```python
import functools

import jax
import jax.numpy as jnp
from jax import lax
from jax.experimental import pallas as pl
from jax.experimental.pallas import tpu as pltpu
from jax.sharding import PartitionSpec as P

VMEM = pl.BlockSpec(memory_space=pltpu.VMEM)
SMEM = pl.BlockSpec(memory_space=pltpu.SMEM)
LANES = 128


def columns_kernel(science_ref, variance_ref, psf_ref, out_ref):
    slots, height, breadth = science_ref.shape
    taps = psf_ref.shape[1]
    radius = taps // 2
    column = lax.broadcasted_iota(jnp.int32, (2 * height, breadth), 1)
    row = lax.broadcasted_iota(jnp.int32, (2 * height, 1), 0)
    for e in range(slots):
        inverse = 1.0 / variance_ref[e]
        pair = jnp.concatenate([science_ref[e] / variance_ref[e], inverse], axis=0)
        summed = jnp.zeros_like(pair)
        for k in range(taps):
            w = psf_ref[e, k]
            weight = jnp.where(row < height, w, w * w)
            reach = k - radius
            moved = pair
            if reach:
                moved = pltpu.roll(pair, (-reach) % breadth, 1)
                inside = column < breadth - reach if reach > 0 else column >= -reach
                moved = jnp.where(inside, moved, 0.0)
            summed = summed + weight * moved
        out_ref[e] = summed


def stack_kernel(order, place_ref, psf_ref, shifts_ref, *refs):
    pieces, outs = refs[:-order], refs[-order:]
    slots, paired, breadth = pieces[0].shape[-3:]
    height = paired // 2
    taps = psf_ref.shape[1]
    radius = taps // 2
    sources = sum(p.shape[0] for p in pieces)
    rows_all = sources * height
    block = rows_all // order
    epoch = place_ref[0]
    mine = place_ref[1]
    depth = sources * slots * paired
    lane = lax.broadcasted_iota(jnp.int32, (paired, LANES), 1)

    def shifted(x, shift):
        tiles = [x[:, i : i + LANES] for i in range(0, breadth, LANES)]
        turn = lax.rem(LANES - shift, LANES)
        turned = [pltpu.roll(t, turn, 1) for t in tiles]
        zero = jnp.zeros_like(turned[0])
        inside = (lane + shift >= 0) & (lane + shift < LANES)
        ahead = jnp.broadcast_to(shift >= 0, lane.shape)
        made = []
        for i, t in enumerate(turned):
            after = turned[i + 1] if i + 1 < len(turned) else zero
            before = turned[i - 1] if i else zero
            made.append(jnp.where(inside, t, jnp.where(ahead, after, before)))
        return jnp.concatenate(made, axis=1)

    images = []
    for p in pieces:
        for s in range(p.shape[0]):
            for e in range(slots):
                images.append(shifted(p[s, e], shifts_ref[0, epoch * slots + e, 0]))
    image = jnp.concatenate(images, axis=0)

    out_at = lax.broadcasted_iota(jnp.int32, (2 * rows_all, 1), 0)
    step = out_at // (2 * block)
    out_member = (out_at // block) % 2
    out_row = (step ^ epoch) * block + out_at % block
    in_at = lax.broadcasted_iota(jnp.int32, (1, depth), 1)
    in_row_local = in_at % height
    in_member = (in_at // height) % 2
    in_slot = (in_at // paired) % slots
    place = in_at // (paired * slots)
    in_source = jnp.zeros_like(place)
    for s in range(sources):
        in_source = jnp.where(place == s, mine ^ place_ref[2 + s], in_source)
    in_row = in_source * height + in_row_local
    shift_row = jnp.zeros_like(in_at)
    for e in range(slots):
        shift_row = jnp.where(in_slot == e, shifts_ref[1, epoch * slots + e, 0], shift_row)
    target = out_row + shift_row
    tap = in_row - target + radius
    matrix = jnp.zeros((2 * rows_all, depth), jnp.float32)
    for k in range(taps):
        weight = jnp.zeros(in_at.shape, jnp.float32)
        for e in range(slots):
            weight = jnp.where(in_slot == e, psf_ref[e, k], weight)
        weight = jnp.where(in_member == 0, weight, weight * weight)
        matrix = jnp.where(tap == k, weight, matrix)
    keep = (target >= 0) & (target < rows_all) & (in_member == out_member)
    matrix = jnp.where(keep, matrix, 0.0)
    product = jnp.dot(
        matrix, image, precision=lax.Precision.HIGHEST, preferred_element_type=jnp.float32
    )
    for k, out in enumerate(outs):
        for m in range(2):
            at = (2 * k + m) * block
            out[m] = product[at : at + block]


def exchange(array, axis, mask):
    count = lax.axis_size(axis)
    return lax.ppermute(array, axis, [(i, i ^ mask) for i in range(count)])


def per_device(science, variance, psf, shifts):
    slots, height, breadth = science.shape
    order = lax.axis_size("epoch")
    sources = lax.axis_size("vel")
    filtered = pl.pallas_call(
        columns_kernel,
        out_shape=jax.ShapeDtypeStruct((slots, 2 * height, breadth), jnp.float32),
        in_specs=[VMEM, VMEM, SMEM],
        out_specs=VMEM,
        name="columns",
    )(science, variance, psf)
    if sources <= 8:
        masks = list(range(0, sources, 2))
        same = jnp.stack([filtered] + [exchange(filtered, "vel", m) for m in masks[1:]])
        pieces = [same, exchange(same, "vel", 1)]
        masks = masks + [m ^ 1 for m in masks]
        mine = lax.axis_index("vel")
    else:
        pieces = [lax.all_gather(filtered, "vel")]
        masks = list(range(sources))
        mine = 0
    place = jnp.stack([jnp.int32(v) for v in [lax.axis_index("epoch"), mine] + masks])
    block = sources * height // order
    chunks = pl.pallas_call(
        functools.partial(stack_kernel, order),
        out_shape=[jax.ShapeDtypeStruct((2, block, breadth), jnp.float32)] * order,
        in_specs=[SMEM] * 3 + [VMEM] * len(pieces),
        out_specs=[VMEM] * order,
        name="stack",
    )(place, psf, shifts, *pieces)
    total = chunks[0]
    for k in range(1, order):
        total = total + exchange(chunks[k], "epoch", k)
    return (total[0] / jnp.sqrt(total[1]))[None]


def solution(mesh):
    return jax.shard_map(
        per_device,
        mesh=mesh,
        in_specs=(
            P("epoch", "vel", None),
            P("epoch", "vel", None),
            P("epoch", None),
            P(None, None, "vel"),
        ),
        out_specs=P("vel", "epoch", None),
        check_vma=False,
    )
```

time: 81.9 us -> 28.8 us (0.35)
  waiting for transfers between devices: 34.8 us -> 10.5 us
  between operations: 19.1 us -> 0.04 us
  blocking collectives: 14.1 us -> 0 us
  starting transfers between devices: 3.69 us -> 8.95 us
  Pallas kernels: 0 us -> 3.95 us
  other arithmetic: 5.5 us -> 2.34 us
  local copies, waits for them, and re-layouts: 4.27 us -> 2.71 us
    unnamed x2 -> x0, waiting for transfers between devices: 34.8 us -> none
    all_gather x1 -> x0, blocking collectives: 14.1 us -> none  [per_device(): gathered = lax.all_gather(filtered, 'vel', axis=2, tiled=True)]
    ppermute x2 -> x7, waiting for transfers between devices: 0.01 us -> 10.5 us  [exchange(): return lax.ppermute(array, axis, [(i, i ^ mask) for i in range(count)])]
    ppermute x2 -> x7, starting transfers between devices: 3.69 us -> 8.95 us  [exchange(): return lax.ppermute(array, axis, [(i, i ^ mask) for i in range(count)])]
    pallas_call x0 -> x2, Pallas kernels: none -> 3.95 us  [the longest x1 2.29 us: per_device(): pl.pallas_call(functools.partial(stack_kernel, order), out_shape=[jax.Sha...]
    slice x2 -> x0, local copies, waits for them, and re-layouts: 2.12 us -> none  [the longest x1 1.38 us: per_device(): local_shifts[0, epoch_slot]]
    another operation x4 -> x1, other arithmetic: 2.58 us -> 0.86 us  [per_device(): jnp.stack([filtered] + [exchange(filtered, 'vel', m) for m in masks[1:]])]
    unnamed x3 -> x7, local copies, waits for them, and re-layouts: 0.59 us -> 2.08 us
  transfers between devices with their start and end apart: 3 -> 7, of which waited for: 1 -> 6; matrix products, arithmetic and copies ran while one was open for 2% -> 5% of each run, Pallas kernels for 0% -> 0%
where the time goes in v1:
time: 28.8 us; the launch traced here: 28.5 us
  waiting for transfers between devices  10.5 us (36%)
  starting transfers between devices  8.95 us (31%)
  Pallas kernels  3.95 us (14%)
  local copies, waits for them, and re-layouts  2.71 us (9%)
  other arithmetic  2.34 us (8%)
    ppermute x7, waiting for transfers between devices, exchange(): return lax.ppermute(array, axis, [(i, i ^ mask) for i in range(count)])  10.5 us
    ppermute x7, starting transfers between devices, exchange(): return lax.ppermute(array, axis, [(i, i ^ mask) for i in range(count)])  8.95 us
    pallas_call x1, Pallas kernels, per_device(): pl.pallas_call(functools.partial(stack_kernel, order), out_shape=[jax.Sha...  2.29 us
    unnamed x7, local copies, waits for them, and re-layouts  2.08 us
    pallas_call x1, Pallas kernels, per_device(): pl.pallas_call(columns_kernel, out_shape=jax.ShapeDtypeStruct((slots, 2 *...  1.66 us
    another operation x1, other arithmetic, per_device(): jnp.stack([filtered] + [exchange(filtered, 'vel', m) for m in masks[1:]])  0.86 us
    add x1, other arithmetic, per_device(): total = total + exchange(chunks[k], 'epoch', k)  0.86 us
    another operation x1, local copies, waits for them, and re-layouts, per_device(): jnp.stack([jnp.int32(v) for v in [lax.axis_index('epoch'), mine] + masks])  0.63 us
  transfers between devices with their start and end apart: 7, of which 6 were waited for; matrix products, arithmetic and copies ran while one was open for 5% of the time, Pallas kernels for 0%

profile of v1, /device:TPU:0, one launch (start us, length us, event | category | flops | bytes accessed | tf_op | source)
XLA Modules:
  0.0 28.5 jit_solution(18209428169453533903)
XLA Ops:
  0.0 1.7 %columns.1 = f32[2,8,1024]{2,1,0:T(8,128)} custom-call(f32[2,4,1024]{2,1,0:T(4,128)} %science_ref.1, f32[2,4,1024]{2,1,0:T(4,128)} %variance_ref.1, f32[2,9]{1,0:T(2,128)} %psf_ref.3), custom_call_target="tpu_custom_call" | custom-call | tf_op jit(solution)/shard_map/columns/pallas_call | solution.py:118
  1.7 3.9 %collective-permute-start.2 = (f32[2,8,1024]{2,1,0:T(8,128)}, f32[2,8,1024]{2,1,0:T(8,128)S(1)}, u32[]{:S(2)}, u32[]{:S(2)}) collective-permute-start(f32[2,8,1024]{2,1,0:T(8,128)} %columns.1), channel_id=1, source_target_pairs={{0,6},{1,7},{2,4},{3,5},{4,2},{5,3},{6,0},{7,1},{8,14},{9,15},{10,... | collective-permute-start | bytes 196616 | tf_op jit(solution)/shard_map/ppermute | solution.py:111
  5.6 0.5 %collective-permute-start.1 = (f32[2,8,1024]{2,1,0:T(8,128)}, f32[2,8,1024]{2,1,0:T(8,128)S(1)}, u32[]{:S(2)}, u32[]{:S(2)}) collective-permute-start(f32[2,8,1024]{2,1,0:T(8,128)} %columns.1), channel_id=1, source_target_pairs={{0,4},{1,5},{2,6},{3,7},{4,0},{5,1},{6,2},{7,3},{8,12},{9,13},{10,... | collective-permute-start | bytes 196616 | tf_op jit(solution)/shard_map/ppermute | solution.py:111
  6.1 0.1 collective-permute-start
  6.1 1.9 %collective-permute-done.2 = f32[2,8,1024]{2,1,0:T(8,128)S(1)} collective-permute-done((f32[2,8,1024]{2,1,0:T(8,128)}, f32[2,8,1024]{2,1,0:T(8,128)S(1)}, u32[]{:S(2)}, u32[]{:S(2)}) %collective-permute-start.2) | collective-permute-done | bytes 65568 | tf_op jit(solution)/shard_map/ppermute | solution.py:111
  8.0 2.0 %collective-permute-done.1 = f32[2,8,1024]{2,1,0:T(8,128)S(1)} collective-permute-done((f32[2,8,1024]{2,1,0:T(8,128)}, f32[2,8,1024]{2,1,0:T(8,128)S(1)}, u32[]{:S(2)}, u32[]{:S(2)}) %collective-permute-start.1) | collective-permute-done | bytes 65568 | tf_op jit(solution)/shard_map/ppermute | solution.py:111
  10.1 0.5 %collective-permute-done = f32[2,8,1024]{2,1,0:T(8,128)S(1)} collective-permute-done((f32[2,8,1024]{2,1,0:T(8,128)}, f32[2,8,1024]{2,1,0:T(8,128)S(1)}, u32[]{:S(2)}, u32[]{:S(2)}) %collective-permute-start) | collective-permute-done | bytes 65568 | tf_op jit(solution)/shard_map/ppermute | solution.py:111
  10.6 0.9 %pad_maximum_fusion.refs_0_ = f32[4,2,8,1024]{3,2,1,0:T(8,128)S(1)} fusion(f32[1,2,8,1024]{3,2,1,0:T(8,128)S(1)} %bitcast.7, f32[1,2,8,1024]{3,2,1,0:T(8,128)S(1)} %bitcast.8, f32[1,2,8,1024]{3,2,1,0:T(8,128)S(1)} %bitcast.9, f32[1,2,8,1024]{3,2,1,0:T(8,128)} %bitcast.6), kind=kLoop, calls=%fused_computation | loop fusion | flops 196608 | bytes 524288 | tf_op jit(solution)/shard_map/stack | solution.py:127
  11.4 0.0 copy-start
  11.4 0.1 collective-permute-start.3
  11.5 0.0 copy-start.2
  11.5 0.7 %copy-done.2 = s32[2,8,1]{1,2,0:T(1,128)S(1)} copy-done((s32[2,8,1]{1,2,0:T(1,128)S(1)}, s32[2,8,1]{1,2,0:T(1,128)}, u32[]{:S(2)}) %copy-start.2) | copy-done | bytes 88
  12.2 0.7 %copy.5.shifts_ref = s32[2,8,1]{2,1,0:T(8,128)} copy(s32[2,8,1]{1,2,0:T(1,128)S(1)} %copy-done.2) | data formatting | bytes 128 | tf_op args[3]
  12.9 0.6 %stack.27.place_ref = s32[10]{0:T(128)} concatenate(s32[1]{0:T(128)} %bitcast, s32[1]{0:T(128)} %bitcast.1, s32[1]{0:T(128)} %constant.4.clone.1, s32[1]{0:T(128)} %constant.5.clone.1, s32[1]{0:T(128)} %constant.6.clone.1, s32[1]{0:T(128)} %constant.7.clone.1, s32[1]{0:T(128)} %constant.8.clone.1, s32[1]{0:T(128)} %constant.9.clone.1, s32[1]{0:T(128)} %constant.22.clone.1, ...), dimensions={0} | concatenate | bytes 80 | tf_op jit(solution)/shard_map/stack | solution.py:135
  13.5 0.0 collective-permute-done.3.refs_1_
  13.5 0.0 copy-done
  13.5 0.0 copy-start.1
  13.5 0.7 %copy-done.1 = f32[4,2,8,1024]{3,2,1,0:T(8,128)} copy-done((f32[4,2,8,1024]{3,2,1,0:T(8,128)}, f32[4,2,8,1024]{3,2,1,0:T(8,128)S(1)}, u32[]{:S(2)}) %copy-start.1) | copy-done | bytes 262168
  14.2 2.3 %stack.33 = (f32[2,8,1024]{2,1,0:T(8,128)}, f32[2,8,1024]{2,1,0:T(8,128)}, f32[2,8,1024]{2,1,0:T(8,128)}, f32[2,8,1024]{2,1,0:T(8,128)}) custom-call(s32[10]{0:T(128)} %stack.27.place_ref, f32[2,9]{1,0:T(2,128)} %psf_ref.3, s32[2,8,1]{2,1,0:T(8,128)} %copy.5.shifts_ref, f32[4,2,8,1024]{3,2,1,0:T(8,128)} %copy-done, f32[4,2,8,1024]{3,2,1,0:T(8,128)} %copy-done.1), custom_call_target="tpu_custom_call" | custom-call | tf_op jit(solution)/shard_map/stack/pallas_call | solution.py:137
  16.5 1.6 %collective-permute-start.4 = (f32[2,8,1024]{2,1,0:T(8,128)}, f32[2,8,1024]{2,1,0:T(8,128)S(1)}, u32[]{:S(2)}, u32[]{:S(2)}) collective-permute-start(f32[2,8,1024]{2,1,0:T(8,128)} %get-tuple-element.10), channel_id=1, source_target_pairs={{0,8},{8,0},{16,24},{24,16},{1,9},{9,1},{17,25},{25,17},{2,10},{10... | collective-permute-start | bytes 196616 | tf_op jit(solution)/shard_map/ppermute | solution.py:111
  18.1 2.6 %collective-permute-start.5 = (f32[2,8,1024]{2,1,0:T(8,128)}, f32[2,8,1024]{2,1,0:T(8,128)S(1)}, u32[]{:S(2)}, u32[]{:S(2)}) collective-permute-start(f32[2,8,1024]{2,1,0:T(8,128)} %get-tuple-element.11), channel_id=1, source_target_pairs={{0,16},{8,24},{16,0},{24,8},{1,17},{9,25},{17,1},{25,9},{2,18},{10... | collective-permute-start | bytes 196616 | tf_op jit(solution)/shard_map/ppermute | solution.py:111
  20.7 0.2 collective-permute-start.6
  20.9 0.3 %collective-permute-done.4 = f32[2,8,1024]{2,1,0:T(8,128)S(1)} collective-permute-done((f32[2,8,1024]{2,1,0:T(8,128)}, f32[2,8,1024]{2,1,0:T(8,128)S(1)}, u32[]{:S(2)}, u32[]{:S(2)}) %collective-permute-start.4) | collective-permute-done | bytes 65568 | tf_op jit(solution)/shard_map/ppermute | solution.py:111
  21.2 4.1 %collective-permute-done.5 = f32[2,8,1024]{2,1,0:T(8,128)S(1)} collective-permute-done((f32[2,8,1024]{2,1,0:T(8,128)}, f32[2,8,1024]{2,1,0:T(8,128)S(1)}, u32[]{:S(2)}, u32[]{:S(2)}) %collective-permute-start.5) | collective-permute-done | bytes 65568 | tf_op jit(solution)/shard_map/ppermute | solution.py:111
  25.3 1.7 %collective-permute-done.6 = f32[2,8,1024]{2,1,0:T(8,128)S(1)} collective-permute-done((f32[2,8,1024]{2,1,0:T(8,128)}, f32[2,8,1024]{2,1,0:T(8,128)S(1)}, u32[]{:S(2)}, u32[]{:S(2)}) %collective-permute-start.6) | collective-permute-done | bytes 65568 | tf_op jit(solution)/shard_map/ppermute | solution.py:111
  27.0 0.9 %add_add_fusion = f32[2,8,1024]{2,1,0:T(8,128)S(1)} fusion(f32[2,8,1024]{2,1,0:T(8,128)S(1)} %collective-permute-done.6, f32[2,8,1024]{2,1,0:T(8,128)S(1)} %collective-permute-done.5, f32[2,8,1024]{2,1,0:T(8,128)} %get-tuple-element.9, f32[2,8,1024]{2,1,0:T(8,128)S(1)} %collective-permute-done.4), kind=kLoop, calls=%fused_computation.1 | loop fusion | flops 49152 | bytes 327680 | tf_op jit(solution)/shard_map/add | solution.py:146
  27.8 0.6 %fusion = f32[1,8,1024]{2,1,0:T(8,128)} fusion(f32[2,8,1024]{2,1,0:T(8,128)S(1)} %add_add_fusion), kind=kLoop, calls=%fused_computation.3 | loop fusion | flops 8192 | bytes 98304 | tf_op jit(solution)/shard_map/div | solution.py:147
Async XLA Ops:
  1.7 6.4 %collective-permute-start.2 = (f32[2,8,1024]{2,1,0:T(8,128)}, f32[2,8,1024]{2,1,0:T(8,128)S(1)}, u32[]{:S(2)}, u32[]{:S(2)}) collective-permute-start(f32[2,8,1024]{2,1,0:T(8,128)} %columns.1), channel_id=1, source_target_pairs={{0,6},{1,7},{2,4},{3,5},{4,2},{5,3},{6,0},{7,1},{8,14},{9,15},{10,... | collective-permute-start | bytes 196616 | tf_op jit(solution)/shard_map/ppermute | solution.py:111
  5.6 4.5 %collective-permute-start.1 = (f32[2,8,1024]{2,1,0:T(8,128)}, f32[2,8,1024]{2,1,0:T(8,128)S(1)}, u32[]{:S(2)}, u32[]{:S(2)}) collective-permute-start(f32[2,8,1024]{2,1,0:T(8,128)} %columns.1), channel_id=1, source_target_pairs={{0,4},{1,5},{2,6},{3,7},{4,0},{5,1},{6,2},{7,3},{8,12},{9,13},{10,... | collective-permute-start | bytes 196616 | tf_op jit(solution)/shard_map/ppermute | solution.py:111
  6.1 4.5 %collective-permute-start = (f32[2,8,1024]{2,1,0:T(8,128)}, f32[2,8,1024]{2,1,0:T(8,128)S(1)}, u32[]{:S(2)}, u32[]{:S(2)}) collective-permute-start(f32[2,8,1024]{2,1,0:T(8,128)} %columns.1), channel_id=1, source_target_pairs={{0,2},{1,3},{2,0},{3,1},{4,6},{5,7},{6,4},{7,5},{8,10},{9,11},{10,... | collective-permute-start | bytes 196616 | tf_op jit(solution)/shard_map/ppermute | solution.py:111
  11.4 2.1 %copy-start = (f32[4,2,8,1024]{3,2,1,0:T(8,128)}, f32[4,2,8,1024]{3,2,1,0:T(8,128)S(1)}, u32[]{:S(2)}) copy-start(f32[4,2,8,1024]{3,2,1,0:T(8,128)S(1)} %pad_maximum_fusion.refs_0_) | copy-start | bytes 786436
  11.4 2.1 %collective-permute-start.3 = (f32[4,2,8,1024]{3,2,1,0:T(8,128)S(1)}, f32[4,2,8,1024]{3,2,1,0:T(8,128)S(1)}, u32[]{:S(2)}, u32[]{:S(2)}) collective-permute-start(f32[4,2,8,1024]{3,2,1,0:T(8,128)S(1)} %pad_maximum_fusion.refs_0_), channel_id=1, source_target_pairs={{0,1},{1,0},{2,3},{3,2},{4,5},{5,4},{6,7},{7,6},{8,9},{9,8},{10,11... | collective-permute-start | bytes 786440 | tf_op jit(solution)/shard_map/ppermute | solution.py:111
  11.5 0.7 %copy-start.2 = (s32[2,8,1]{1,2,0:T(1,128)S(1)}, s32[2,8,1]{1,2,0:T(1,128)}, u32[]{:S(2)}) copy-start(s32[2,8,1]{1,2,0:T(1,128)} %param.7) | copy-start | bytes 196
  13.5 0.7 %copy-start.1 = (f32[4,2,8,1024]{3,2,1,0:T(8,128)}, f32[4,2,8,1024]{3,2,1,0:T(8,128)S(1)}, u32[]{:S(2)}) copy-start(f32[4,2,8,1024]{3,2,1,0:T(8,128)S(1)} %collective-permute-done.3.refs_1_) | copy-start | bytes 786436
  16.5 4.7 %collective-permute-start.4 = (f32[2,8,1024]{2,1,0:T(8,128)}, f32[2,8,1024]{2,1,0:T(8,128)S(1)}, u32[]{:S(2)}, u32[]{:S(2)}) collective-permute-start(f32[2,8,1024]{2,1,0:T(8,128)} %get-tuple-element.10), channel_id=1, source_target_pairs={{0,8},{8,0},{16,24},{24,16},{1,9},{9,1},{17,25},{25,17},{2,10},{10... | collective-permute-start | bytes 196616 | tf_op jit(solution)/shard_map/ppermute | solution.py:111
  18.1 7.2 %collective-permute-start.5 = (f32[2,8,1024]{2,1,0:T(8,128)}, f32[2,8,1024]{2,1,0:T(8,128)S(1)}, u32[]{:S(2)}, u32[]{:S(2)}) collective-permute-start(f32[2,8,1024]{2,1,0:T(8,128)} %get-tuple-element.11), channel_id=1, source_target_pairs={{0,16},{8,24},{16,0},{24,8},{1,17},{9,25},{17,1},{25,9},{2,18},{10... | collective-permute-start | bytes 196616 | tf_op jit(solution)/shard_map/ppermute | solution.py:111
  20.7 6.3 %collective-permute-start.6 = (f32[2,8,1024]{2,1,0:T(8,128)}, f32[2,8,1024]{2,1,0:T(8,128)S(1)}, u32[]{:S(2)}, u32[]{:S(2)}) collective-permute-start(f32[2,8,1024]{2,1,0:T(8,128)} %get-tuple-element.12), channel_id=1, source_target_pairs={{0,24},{8,16},{16,8},{24,0},{1,25},{9,17},{17,9},{25,1},{2,26},{10... | collective-permute-start | bytes 196616 | tf_op jit(solution)/shard_map/ppermute | solution.py:111

commit v2 on v1

v2 whole, which is shorter than its diff:
```python
import functools

import jax
import jax.numpy as jnp
from jax import lax
from jax.experimental import pallas as pl
from jax.experimental.pallas import tpu as pltpu
from jax.sharding import PartitionSpec as P


VMEM = pl.BlockSpec(memory_space=pltpu.VMEM)
SMEM = pl.BlockSpec(memory_space=pltpu.SMEM)
HBM = pl.BlockSpec(memory_space=pltpu.HBM)
LANES = 128


def tiles_of(x):
    return [x[:, i : i + LANES] for i in range(0, x.shape[1], LANES)]


def columns_kernel(science_hbm, variance_hbm, psf_hbm, out_ref, science, variance, psf, sems):
    copies = [
        pltpu.make_async_copy(source, target, sems.at[i])
        for i, (source, target) in enumerate(
            ((variance_hbm, variance), (science_hbm, science), (psf_hbm, psf))
        )
    ]
    for copy in copies:
        copy.start()
    slots, height, _ = science.shape
    taps = psf.shape[1]
    radius = taps // 2
    lane = lax.broadcasted_iota(jnp.int32, (2 * height, LANES), 1)
    psi_row = lax.broadcasted_iota(jnp.int32, (2 * height, LANES), 0) < height
    for copy in copies:
        copy.wait()
    for e in range(slots):
        inverse = 1.0 / variance[e]
        pair = tiles_of(jnp.concatenate([science[e] * inverse, inverse], axis=0))
        zero = jnp.zeros_like(pair[0])
        summed = [zero] * len(pair)
        for k in range(taps):
            w = psf[e, k]
            weight = jnp.where(psi_row, w, w * w)
            reach = k - radius
            moved = pair
            if reach:
                turned = [pltpu.roll(t, (-reach) % LANES, 1) for t in pair]
                if reach > 0:
                    moved = [jnp.where(lane < LANES - reach, a, b) for a, b in zip(turned, turned[1:] + [zero])]
                else:
                    moved = [jnp.where(lane >= -reach, a, b) for a, b in zip(turned, [zero] + turned[:-1])]
            summed = [s + weight * m for s, m in zip(summed, moved)]
        out_ref[e] = jnp.concatenate(summed, axis=1)


def banded(order, masks, relative, height, slots, psf_ref, shifts_ref):
    taps = psf_ref.shape[1]
    radius = taps // 2
    sources = len(masks)
    paired = 2 * height
    rows_all = sources * height
    block = rows_all // order
    depth = sources * slots * paired
    epoch = lax.axis_index("epoch")
    mine = lax.axis_index("vel") if relative else 0
    out_at = lax.broadcasted_iota(jnp.int32, (2 * rows_all, 1), 0)
    step = out_at // (2 * block)
    out_member = (out_at // block) % 2
    out_row = (step ^ epoch) * block + out_at % block
    in_at = lax.broadcasted_iota(jnp.int32, (1, depth), 1)
    in_member = (in_at // height) % 2
    in_slot = (in_at // paired) % slots
    place = in_at // (paired * slots)
    in_source = jnp.zeros_like(place)
    for s, mask in enumerate(masks):
        in_source = jnp.where(place == s, mine ^ mask, in_source)
    in_row = in_source * height + in_at % height
    shift_row = jnp.zeros_like(in_at)
    for e in range(slots):
        shift_row = jnp.where(in_slot == e, shifts_ref[1, epoch * slots + e], shift_row)
    target = out_row + shift_row
    tap = in_row - target + radius
    matrix = jnp.zeros((2 * rows_all, depth), jnp.float32)
    for k in range(taps):
        weight = jnp.zeros(in_at.shape, jnp.float32)
        for e in range(slots):
            weight = jnp.where(in_slot == e, psf_ref[e, k], weight)
        weight = jnp.where(in_member == 0, weight, weight * weight)
        matrix = jnp.where(tap == k, weight, matrix)
    keep = (target >= 0) & (target < rows_all) & (in_member == out_member)
    return jnp.where(keep, matrix, 0.0)


def split(x):
    high = x.astype(jnp.bfloat16)
    return high, (x - high.astype(jnp.float32)).astype(jnp.bfloat16)


def shifted(x, shift):
    tiles = tiles_of(x)
    lane = lax.broadcasted_iota(jnp.int32, tiles[0].shape, 1)
    turned = [pltpu.roll(t, lax.rem(LANES - shift, LANES), 1) for t in tiles]
    zero = jnp.zeros_like(turned[0])
    inside = (lane + shift >= 0) & (lane + shift < LANES)
    ahead = jnp.broadcast_to(shift, lane.shape) >= 0
    made = []
    for before, t, after in zip([zero] + turned[:-1], turned, turned[1:] + [zero]):
        made.append(jnp.where(inside, t, jnp.where(ahead, after, before)))
    return jnp.concatenate(made, axis=1)


def product_of(pieces, shifts, high, low):
    images = [shifted(p[s, e], shift) for p in pieces for s in range(p.shape[0]) for e, shift in enumerate(shifts)]
    image_high, image_low = split(jnp.concatenate(images, axis=0))
    dot = functools.partial(jnp.dot, preferred_element_type=jnp.float32)
    return dot(high, image_high) + dot(high, image_low) + dot(low, image_high)


def store_blocks(product, outs):
    at = 0
    for out in outs:
        rows = out.shape[-2]
        for m in range(out.shape[0]):
            out[m] = product[at : at + rows]
            at += rows


def matrix_kernel(order, masks, height, psf_ref, shifts_ref, high_ref, low_ref, column_ref):
    slots = column_ref.shape[0]
    matrix = banded(order, masks, True, height, slots, psf_ref, shifts_ref)
    high_ref[...], low_ref[...] = split(matrix)
    epoch = lax.axis_index("epoch")
    for e in range(slots):
        shift = shifts_ref[0, epoch * slots + e]
        column_ref[e] = jnp.full(column_ref.shape[1:], shift, jnp.int32)


def partial_product(pieces, start, high_ref, low_ref, column_ref):
    slots, paired = pieces[0].shape[1:3]
    stop = start + sum(p.shape[0] for p in pieces) * slots * paired
    shifts = [column_ref[e][0, 0] for e in range(slots)]
    return product_of(pieces, shifts, high_ref[:, start:stop], low_ref[:, start:stop])


def early_kernel(high_ref, low_ref, column_ref, pieces_ref, partial_ref):
    partial_ref[...] = partial_product([pieces_ref], 0, high_ref, low_ref, column_ref)


def late_kernel(high_ref, low_ref, column_ref, partial_ref, pieces_ref, *outs):
    start = high_ref.shape[1] // 2
    product = partial_product([pieces_ref], start, high_ref, low_ref, column_ref)
    store_blocks(partial_ref[...] + product, outs)


def whole_kernel(order, masks, psf_ref, shifts_ref, pieces_ref, *outs):
    slots, paired = pieces_ref.shape[1:3]
    high, low = split(banded(order, masks, False, paired // 2, slots, psf_ref, shifts_ref))
    epoch = lax.axis_index("epoch")
    shifts = [shifts_ref[0, epoch * slots + e] for e in range(slots)]
    store_blocks(product_of([pieces_ref], shifts, high, low), outs)


def grant(bytes_used):
    return pltpu.CompilerParams(vmem_limit_bytes=min(4 * bytes_used, 60 << 20))


def exchange(array, axis, mask):
    count = lax.axis_size(axis)
    return lax.ppermute(array, axis, [(i, i ^ mask) for i in range(count)])


def per_device(science, variance, psf, shifts):
    slots, height, breadth = science.shape
    order = lax.axis_size("epoch")
    sources = lax.axis_size("vel")
    paired = 2 * height
    shifts = shifts.reshape(shifts.shape[:2])
    filtered = pl.pallas_call(
        columns_kernel,
        out_shape=jax.ShapeDtypeStruct((slots, paired, breadth), jnp.float32),
        in_specs=[HBM, HBM, HBM],
        out_specs=VMEM,
        scratch_shapes=[
            pltpu.VMEM(science.shape, jnp.float32),
            pltpu.VMEM(science.shape, jnp.float32),
            pltpu.SMEM(psf.shape, jnp.float32),
            pltpu.SemaphoreType.DMA((3,)),
        ],
        compiler_params=grant(16 * science.size),
        name="columns",
    )(*(pltpu.with_memory_space_constraint(a, pltpu.HBM) for a in (science, variance, psf)))
    rows_all = sources * height
    block = rows_all // order
    depth = sources * slots * paired
    used = grant(4 * (sources * filtered.size + 2 * rows_all * (depth + breadth)))
    chunk = jax.ShapeDtypeStruct((2, block, breadth), jnp.float32)
    if sources == 8:
        across = exchange(filtered, "vel", 6)
        along = exchange(filtered, "vel", 4)
        aside = exchange(filtered, "vel", 2)
        own = jnp.stack([filtered, across, along, aside])
        twin = exchange(own, "vel", 1)
        masks = [0, 6, 4, 2, 1, 7, 5, 3]
        state = pl.pallas_call(
            functools.partial(matrix_kernel, order, masks, height),
            out_shape=[
                jax.ShapeDtypeStruct((2 * rows_all, depth), jnp.bfloat16),
                jax.ShapeDtypeStruct((2 * rows_all, depth), jnp.bfloat16),
                jax.ShapeDtypeStruct((slots, 8, LANES), jnp.int32),
            ],
            in_specs=[SMEM] * 2,
            out_specs=[VMEM] * 3,
            compiler_params=used,
            name="matrix",
        )(psf, shifts)
        partial = pl.pallas_call(
            early_kernel,
            out_shape=jax.ShapeDtypeStruct((2 * rows_all, breadth), jnp.float32),
            in_specs=[VMEM] * 4,
            out_specs=VMEM,
            compiler_params=used,
            name="early",
        )(*state, own)
        chunks = pl.pallas_call(
            late_kernel,
            out_shape=[chunk] * order,
            in_specs=[VMEM] * 5,
            out_specs=[VMEM] * order,
            compiler_params=used,
            name="late",
        )(*state, partial, twin)
    else:
        chunks = pl.pallas_call(
            functools.partial(whole_kernel, order, list(range(sources))),
            out_shape=[chunk] * order,
            in_specs=[SMEM] * 2 + [VMEM],
            out_specs=[VMEM] * order,
            compiler_params=used,
            name="stack",
        )(psf, shifts, lax.all_gather(filtered, "vel"))
    terms = [chunks[0]] + [exchange(chunks[k], "epoch", k) for k in range(1, order)]
    psi, phi = (sum(t[m] for t in terms) for m in range(2))
    return (psi / jnp.sqrt(phi))[None]


def solution(mesh):
    return jax.shard_map(
        per_device,
        mesh=mesh,
        in_specs=(
            P("epoch", "vel", None),
            P("epoch", "vel", None),
            P("epoch", None),
            P(None, None, "vel"),
        ),
        out_specs=P("vel", "epoch", None),
        check_vma=False,
    )
```

time: 28.8 us -> 24.2 us (0.84)
  local copies, waits for them, and re-layouts: 2.71 us -> 0.6 us
  other arithmetic: 2.34 us -> 0.66 us
  Pallas kernels: 3.95 us -> 2.47 us
  waiting for transfers between devices: 10.5 us -> 11.1 us
    unnamed x7 -> x4, local copies, waits for them, and re-layouts: 2.08 us -> 0.6 us
    pallas_call x2 -> x4, Pallas kernels: 3.95 us -> 2.47 us  [the longest x1 1.06 us: per_device(): pl.pallas_call(columns_kernel, out_shape=jax.ShapeDtypeStruct((slots, pai...]
    add x1 -> x0, other arithmetic: 0.86 us -> none  [per_device(): total = total + exchange(chunks[k], 'epoch', k)]
    another operation x1, other arithmetic: 0.86 us -> 0.02 us  [per_device(): own = jnp.stack([filtered, across, along, aside])]
    another operation x1 -> x0, local copies, waits for them, and re-layouts: 0.63 us -> none  [per_device(): jnp.stack([jnp.int32(v) for v in [lax.axis_index('epoch'), mine] + masks])]
    ppermute x7, waiting for transfers between devices: 10.5 us -> 11.1 us  [exchange(): return lax.ppermute(array, axis, [(i, i ^ mask) for i in range(count)])]
  transfers between devices with their start and end apart: 7 -> 7, of which waited for: 6 -> 5; matrix products, arithmetic and copies ran while one was open for 5% -> 0% of each run, Pallas kernels for 0% -> 4%
where the time goes in v2:
time: 24.2 us; the launch traced here: 24 us
  waiting for transfers between devices  11.1 us (46%)
  starting transfers between devices  9.1 us (38%)
  Pallas kernels  2.47 us (10%)
  other arithmetic  0.66 us (3%)
  local copies, waits for them, and re-layouts  0.6 us (2%)
    ppermute x7, waiting for transfers between devices, exchange(): return lax.ppermute(array, axis, [(i, i ^ mask) for i in range(count)])  11.1 us
    ppermute x7, starting transfers between devices, exchange(): return lax.ppermute(array, axis, [(i, i ^ mask) for i in range(count)])  9.1 us
    pallas_call x1, Pallas kernels, per_device(): pl.pallas_call(columns_kernel, out_shape=jax.ShapeDtypeStruct((slots, pai...  1.06 us
    div x1, other arithmetic, per_device(): return (psi / jnp.sqrt(phi))[None]  0.63 us
    pallas_call x1, Pallas kernels, per_device(): pl.pallas_call(functools.partial(matrix_kernel, order, masks, height), ou...  0.63 us
    unnamed x4, local copies, waits for them, and re-layouts  0.6 us
  transfers between devices with their start and end apart: 7, of which 5 were waited for; matrix products, arithmetic and copies ran while one was open for 0% of the time, Pallas kernels for 4%

profile of v2, /device:TPU:0, one launch (start us, length us, event | category | flops | bytes accessed | tf_op | source)
XLA Modules:
  0.0 24.0 jit_solution(17277441226559713102)
XLA Ops:
  0.0 1.1 %columns.1 = f32[2,8,1024]{2,1,0:T(8,128)S(1)} custom-call(f32[2,4,1024]{2,1,0:T(4,128)} %science_hbm.1, f32[2,4,1024]{2,1,0:T(4,128)} %variance_hbm.1, f32[2,9]{1,0:T(2,128)} %psf_hbm.1), custom_call_target="tpu_custom_call" | custom-call | tf_op jit(solution)/shard_map/columns/pallas_call | solution.py:179
  1.1 3.0 %collective-permute-start.2 = (f32[2,8,1024]{2,1,0:T(8,128)S(1)}, f32[2,8,1024]{2,1,0:T(8,128)S(1)}, u32[]{:S(2)}, u32[]{:S(2)}) collective-permute-start(f32[2,8,1024]{2,1,0:T(8,128)S(1)} %columns.1), channel_id=1, source_target_pairs={{0,2},{1,3},{2,0},{3,1},{4,6},{5,7},{6,4},{7,5},{8,10},{9,11},{10,... | collective-permute-start | bytes 196616 | tf_op jit(solution)/shard_map/ppermute | solution.py:170
  4.1 1.5 %collective-permute-start.1 = (f32[2,8,1024]{2,1,0:T(8,128)S(1)}, f32[2,8,1024]{2,1,0:T(8,128)S(1)}, u32[]{:S(2)}, u32[]{:S(2)}) collective-permute-start(f32[2,8,1024]{2,1,0:T(8,128)S(1)} %columns.1), channel_id=1, source_target_pairs={{0,4},{1,5},{2,6},{3,7},{4,0},{5,1},{6,2},{7,3},{8,12},{9,13},{10,... | collective-permute-start | bytes 196616 | tf_op jit(solution)/shard_map/ppermute | solution.py:170
  5.6 0.0 collective-permute-start
  5.6 0.8 %collective-permute-done.2 = f32[2,8,1024]{2,1,0:T(8,128)S(1)} collective-permute-done((f32[2,8,1024]{2,1,0:T(8,128)S(1)}, f32[2,8,1024]{2,1,0:T(8,128)S(1)}, u32[]{:S(2)}, u32[]{:S(2)}) %collective-permute-start.2) | collective-permute-done | bytes 65568 | tf_op jit(solution)/shard_map/ppermute | solution.py:170
  6.5 1.9 %collective-permute-done.1 = f32[2,8,1024]{2,1,0:T(8,128)S(1)} collective-permute-done((f32[2,8,1024]{2,1,0:T(8,128)S(1)}, f32[2,8,1024]{2,1,0:T(8,128)S(1)}, u32[]{:S(2)}, u32[]{:S(2)}) %collective-permute-start.1) | collective-permute-done | bytes 65568 | tf_op jit(solution)/shard_map/ppermute | solution.py:170
  8.4 2.4 %collective-permute-done = f32[2,8,1024]{2,1,0:T(8,128)S(1)} collective-permute-done((f32[2,8,1024]{2,1,0:T(8,128)S(1)}, f32[2,8,1024]{2,1,0:T(8,128)S(1)}, u32[]{:S(2)}, u32[]{:S(2)}) %collective-permute-start) | collective-permute-done | bytes 65568 | tf_op jit(solution)/shard_map/ppermute | solution.py:170
  10.8 0.0 copy-start.1
  10.8 0.0 copy-start
  10.8 0.1 collective-permute-start.3
  10.9 0.6 %copy-done.1 = s32[2,8,1]{1,2,0:T(1,128)S(1)} copy-done((s32[2,8,1]{1,2,0:T(1,128)S(1)}, s32[2,8,1]{1,2,0:T(1,128)}, u32[]{:S(2)}) %copy-start.1) | copy-done | bytes 88
  11.5 0.0 copy-done
  11.5 0.6 %matrix.1 = (bf16[64,128]{1,0:T(8,128)(2,1)S(1)}, bf16[64,128]{1,0:T(8,128)(2,1)S(1)}, s32[2,8,128]{2,1,0:T(8,128)S(1)}) custom-call(f32[2,9]{1,0:T(2,128)S(1)} %copy-done, s32[2,8]{1,0:T(2,128)S(1)} %bitcast.6), custom_call_target="tpu_custom_call" | custom-call | tf_op jit(solution)/shard_map/matrix/pallas_call | solution.py:205
  12.1 0.4 %early.1.partial_ref = f32[64,1024]{1,0:T(8,128)S(1)} custom-call(bf16[64,128]{1,0:T(8,128)(2,1)S(1)} %get-tuple-element.12.high_ref, bf16[64,128]{1,0:T(8,128)(2,1)S(1)} %get-tuple-element.13.low_ref, s32[2,8,128]{2,1,0:T(8,128)S(1)} %get-tuple-element.14.column_ref, f32[4,2,8,1024]{3,2,1,0:T(8,128)S(1)} %pad_maximum_fusion.pieces_ref), custom_call_target="tpu_custom_call" | custom-call | tf_op jit(solution)/shard_map/early/pallas_call | solution.py:217
  12.5 0.0 collective-permute-done.3.pieces_ref
  12.5 0.4 %late.1 = (f32[2,8,1024]{2,1,0:T(8,128)S(1)}, f32[2,8,1024]{2,1,0:T(8,128)S(1)}, f32[2,8,1024]{2,1,0:T(8,128)S(1)}, f32[2,8,1024]{2,1,0:T(8,128)S(1)}) custom-call(bf16[64,128]{1,0:T(8,128)(2,1)S(1)} %get-tuple-element.12.high_ref, bf16[64,128]{1,0:T(8,128)(2,1)S(1)} %get-tuple-element.13.low_ref, s32[2,8,128]{2,1,0:T(8,128)S(1)} %get-tuple-element.14.column_ref, ...), custom_call_target="tpu_custom_call" | custom-call | tf_op jit(solution)/shard_map/late/pallas_call | solution.py:225
  12.9 1.6 %collective-permute-start.4 = (f32[2,8,1024]{2,1,0:T(8,128)S(1)}, f32[2,8,1024]{2,1,0:T(8,128)S(1)}, u32[]{:S(2)}, u32[]{:S(2)}) collective-permute-start(f32[2,8,1024]{2,1,0:T(8,128)S(1)} %get-tuple-element.16), channel_id=1, source_target_pairs={{0,8},{8,0},{16,24},{24,16},{1,9},{9,1},{17,25},{25,17},{2,10},{10... | collective-permute-start | bytes 196616 | tf_op jit(solution)/shard_map/ppermute | solution.py:170
  14.6 2.6 %collective-permute-start.5 = (f32[2,8,1024]{2,1,0:T(8,128)S(1)}, f32[2,8,1024]{2,1,0:T(8,128)S(1)}, u32[]{:S(2)}, u32[]{:S(2)}) collective-permute-start(f32[2,8,1024]{2,1,0:T(8,128)S(1)} %get-tuple-element.17), channel_id=1, source_target_pairs={{0,16},{8,24},{16,0},{24,8},{1,17},{9,25},{17,1},{25,9},{2,18},{10... | collective-permute-start | bytes 196616 | tf_op jit(solution)/shard_map/ppermute | solution.py:170
  17.2 0.2 collective-permute-start.6
  17.4 0.0 collective-permute-done.4
  17.4 4.7 %collective-permute-done.5 = f32[2,8,1024]{2,1,0:T(8,128)S(1)} collective-permute-done((f32[2,8,1024]{2,1,0:T(8,128)S(1)}, f32[2,8,1024]{2,1,0:T(8,128)S(1)}, u32[]{:S(2)}, u32[]{:S(2)}) %collective-permute-start.5) | collective-permute-done | bytes 65568 | tf_op jit(solution)/shard_map/ppermute | solution.py:170
  22.0 1.3 %collective-permute-done.6 = f32[2,8,1024]{2,1,0:T(8,128)S(1)} collective-permute-done((f32[2,8,1024]{2,1,0:T(8,128)S(1)}, f32[2,8,1024]{2,1,0:T(8,128)S(1)}, u32[]{:S(2)}, u32[]{:S(2)}) %collective-permute-start.6) | collective-permute-done | bytes 65568 | tf_op jit(solution)/shard_map/ppermute | solution.py:170
  23.3 0.6 %fusion.1 = f32[1,8,1024]{2,1,0:T(8,128)} fusion(f32[2,8,1024]{2,1,0:T(8,128)S(1)} %collective-permute-done.6, f32[2,8,1024]{2,1,0:T(8,128)S(1)} %collective-permute-done.5, f32[2,8,1024]{2,1,0:T(8,128)S(1)} %collective-permute-done.4, f32[2,8,1024]{2,1,0:T(8,128)S(1)} %get-tuple-element.15), kind=kLoop, calls=%fused_computation.3 | loop fusion | flops 57344 | bytes 294912 | tf_op jit(solution)/shard_map/div | solution.py:244
  (1 shorter events, 0.0 us)
Async XLA Ops:
  1.1 5.4 %collective-permute-start.2 = (f32[2,8,1024]{2,1,0:T(8,128)S(1)}, f32[2,8,1024]{2,1,0:T(8,128)S(1)}, u32[]{:S(2)}, u32[]{:S(2)}) collective-permute-start(f32[2,8,1024]{2,1,0:T(8,128)S(1)} %columns.1), channel_id=1, source_target_pairs={{0,2},{1,3},{2,0},{3,1},{4,6},{5,7},{6,4},{7,5},{8,10},{9,11},{10,... | collective-permute-start | bytes 196616 | tf_op jit(solution)/shard_map/ppermute | solution.py:170
  4.1 4.3 %collective-permute-start.1 = (f32[2,8,1024]{2,1,0:T(8,128)S(1)}, f32[2,8,1024]{2,1,0:T(8,128)S(1)}, u32[]{:S(2)}, u32[]{:S(2)}) collective-permute-start(f32[2,8,1024]{2,1,0:T(8,128)S(1)} %columns.1), channel_id=1, source_target_pairs={{0,4},{1,5},{2,6},{3,7},{4,0},{5,1},{6,2},{7,3},{8,12},{9,13},{10,... | collective-permute-start | bytes 196616 | tf_op jit(solution)/shard_map/ppermute | solution.py:170
  5.6 5.2 %collective-permute-start = (f32[2,8,1024]{2,1,0:T(8,128)S(1)}, f32[2,8,1024]{2,1,0:T(8,128)S(1)}, u32[]{:S(2)}, u32[]{:S(2)}) collective-permute-start(f32[2,8,1024]{2,1,0:T(8,128)S(1)} %columns.1), channel_id=1, source_target_pairs={{0,6},{1,7},{2,4},{3,5},{4,2},{5,3},{6,0},{7,1},{8,14},{9,15},{10,... | collective-permute-start | bytes 196616 | tf_op jit(solution)/shard_map/ppermute | solution.py:170
  10.8 0.7 %copy-start.1 = (s32[2,8,1]{1,2,0:T(1,128)S(1)}, s32[2,8,1]{1,2,0:T(1,128)}, u32[]{:S(2)}) copy-start(s32[2,8,1]{1,2,0:T(1,128)} %param.7) | copy-start | bytes 196
  10.8 0.7 %copy-start = (f32[2,9]{1,0:T(2,128)S(1)}, f32[2,9]{1,0:T(2,128)}, u32[]{:S(2)}) copy-start(f32[2,9]{1,0:T(2,128)} %psf_hbm.1) | copy-start | bytes 220
  10.8 1.7 %collective-permute-start.3 = (f32[4,2,8,1024]{3,2,1,0:T(8,128)S(1)}, f32[4,2,8,1024]{3,2,1,0:T(8,128)S(1)}, u32[]{:S(2)}, u32[]{:S(2)}) collective-permute-start(f32[4,2,8,1024]{3,2,1,0:T(8,128)S(1)} %pad_maximum_fusion.pieces_ref), channel_id=1, source_target_pairs={{0,1},{1,0},{2,3},{3,2},{4,5},{5,4},{6,7},{7,6},{8,9},{9,8},{10,11... | collective-permute-start | bytes 786440 | tf_op jit(solution)/shard_map/ppermute | solution.py:170
  12.9 4.5 %collective-permute-start.4 = (f32[2,8,1024]{2,1,0:T(8,128)S(1)}, f32[2,8,1024]{2,1,0:T(8,128)S(1)}, u32[]{:S(2)}, u32[]{:S(2)}) collective-permute-start(f32[2,8,1024]{2,1,0:T(8,128)S(1)} %get-tuple-element.16), channel_id=1, source_target_pairs={{0,8},{8,0},{16,24},{24,16},{1,9},{9,1},{17,25},{25,17},{2,10},{10... | collective-permute-start | bytes 196616 | tf_op jit(solution)/shard_map/ppermute | solution.py:170
  14.6 7.5 %collective-permute-start.5 = (f32[2,8,1024]{2,1,0:T(8,128)S(1)}, f32[2,8,1024]{2,1,0:T(8,128)S(1)}, u32[]{:S(2)}, u32[]{:S(2)}) collective-permute-start(f32[2,8,1024]{2,1,0:T(8,128)S(1)} %get-tuple-element.17), channel_id=1, source_target_pairs={{0,16},{8,24},{16,0},{24,8},{1,17},{9,25},{17,1},{25,9},{2,18},{10... | collective-permute-start | bytes 196616 | tf_op jit(solution)/shard_map/ppermute | solution.py:170
  17.2 6.2 %collective-permute-start.6 = (f32[2,8,1024]{2,1,0:T(8,128)S(1)}, f32[2,8,1024]{2,1,0:T(8,128)S(1)}, u32[]{:S(2)}, u32[]{:S(2)}) collective-permute-start(f32[2,8,1024]{2,1,0:T(8,128)S(1)} %get-tuple-element.18), channel_id=1, source_target_pairs={{0,24},{8,16},{16,8},{24,0},{1,25},{9,17},{17,9},{25,1},{2,26},{10... | collective-permute-start | bytes 196616 | tf_op jit(solution)/shard_map/ppermute | solution.py:170

commit v3 on v2

--- a/solution.py
+++ b/solution.py
@@ -12,6 +12,8 @@
 SMEM = pl.BlockSpec(memory_space=pltpu.SMEM)
 HBM = pl.BlockSpec(memory_space=pltpu.HBM)
 LANES = 128
+ROUNDS = ((1, 2, 3, 0), (3, 0, 1, 2), (2, 3, 0, 1))
+RING = (0, 1, 3, 2)
 
 
 def tiles_of(x):
@@ -54,27 +56,38 @@
         out_ref[e] = jnp.concatenate(summed, axis=1)
 
 
-def banded(order, masks, relative, height, slots, psf_ref, shifts_ref):
+def chosen(values, index):
+    if len(set(values)) == 1:
+        return jnp.int32(values[0])
+    return sum(jnp.where(index == i, jnp.int32(v), 0) for i, v in enumerate(values))
+
+
+def banded(ring, origins, height, slots, psf_ref, shifts_ref):
     taps = psf_ref.shape[1]
     radius = taps // 2
-    sources = len(masks)
+    sources = len(origins)
     paired = 2 * height
     rows_all = sources * height
+    order = len(ring)
     block = rows_all // order
     depth = sources * slots * paired
     epoch = lax.axis_index("epoch")
-    mine = lax.axis_index("vel") if relative else 0
+    mine = lax.axis_index("vel")
     out_at = lax.broadcasted_iota(jnp.int32, (2 * rows_all, 1), 0)
     step = out_at // (2 * block)
     out_member = (out_at // block) % 2
-    out_row = (step ^ epoch) * block + out_at % block
+    out_block = jnp.zeros_like(step)
+    for k in range(order):
+        target = chosen([target_of(ring, k, i) for i in range(order)], epoch)
+        out_block = jnp.where(step == k, target, out_block)
+    out_row = out_block * block + out_at % block
     in_at = lax.broadcasted_iota(jnp.int32, (1, depth), 1)
     in_member = (in_at // height) % 2
     in_slot = (in_at // paired) % slots
     place = in_at // (paired * slots)
     in_source = jnp.zeros_like(place)
-    for s, mask in enumerate(masks):
-        in_source = jnp.where(place == s, mine ^ mask, in_source)
+    for s, row in enumerate(origins):
+        in_source = jnp.where(place == s, chosen(row, mine), in_source)
     in_row = in_source * height + in_at % height
     shift_row = jnp.zeros_like(in_at)
     for e in range(slots):
@@ -110,11 +123,15 @@
     return jnp.concatenate(made, axis=1)
 
 
-def product_of(pieces, shifts, high, low):
+def parts_of(matrix):
+    high, low = split(matrix)
+    return jnp.concatenate([high, high, low], axis=1)
+
+
+def product_of(parts, pieces, shifts):
     images = [shifted(p[s, e], shift) for p in pieces for s in range(p.shape[0]) for e, shift in enumerate(shifts)]
-    image_high, image_low = split(jnp.concatenate(images, axis=0))
-    dot = functools.partial(jnp.dot, preferred_element_type=jnp.float32)
-    return dot(high, image_high) + dot(high, image_low) + dot(low, image_high)
+    high, low = split(jnp.concatenate(images, axis=0))
+    return jnp.dot(parts, jnp.concatenate([high, low, high], axis=0), preferred_element_type=jnp.float32)
 
 
 def store_blocks(product, outs):
@@ -126,54 +143,61 @@
             at += rows
 
 
-def matrix_kernel(order, masks, height, psf_ref, shifts_ref, high_ref, low_ref, column_ref):
+def matrix_kernel(ring, origins, height, psf_ref, shifts_ref, column_ref, *parts_refs):
     slots = column_ref.shape[0]
-    matrix = banded(order, masks, True, height, slots, psf_ref, shifts_ref)
-    high_ref[...], low_ref[...] = split(matrix)
+    matrix = banded(ring, origins, height, slots, psf_ref, shifts_ref)
+    at = 0
+    for ref in parts_refs:
+        depth = ref.shape[1] // 3
+        ref[...] = parts_of(matrix[:, at : at + depth])
+        at += depth
     epoch = lax.axis_index("epoch")
     for e in range(slots):
         shift = shifts_ref[0, epoch * slots + e]
         column_ref[e] = jnp.full(column_ref.shape[1:], shift, jnp.int32)
 
 
-def partial_product(pieces, start, high_ref, low_ref, column_ref):
-    slots, paired = pieces[0].shape[1:3]
-    stop = start + sum(p.shape[0] for p in pieces) * slots * paired
-    shifts = [column_ref[e][0, 0] for e in range(slots)]
-    return product_of(pieces, shifts, high_ref[:, start:stop], low_ref[:, start:stop])
-
-
-def early_kernel(high_ref, low_ref, column_ref, pieces_ref, partial_ref):
-    partial_ref[...] = partial_product([pieces_ref], 0, high_ref, low_ref, column_ref)
-
-
-def late_kernel(high_ref, low_ref, column_ref, partial_ref, pieces_ref, *outs):
-    start = high_ref.shape[1] // 2
-    product = partial_product([pieces_ref], start, high_ref, low_ref, column_ref)
-    store_blocks(partial_ref[...] + product, outs)
-
-
-def whole_kernel(order, masks, psf_ref, shifts_ref, pieces_ref, *outs):
+def stack_kernel(count, added, column_ref, parts_ref, *refs):
+    pieces, refs = refs[:count], refs[count:]
+    shifts = [column_ref[e][0, 0] for e in range(column_ref.shape[0])]
+    product = product_of(parts_ref[...], pieces, shifts)
+    if added:
+        product, refs = refs[0][...] + product, refs[1:]
+    if len(refs) == 1:
+        refs[0][...] = product
+    else:
+        store_blocks(product, refs)
+
+
+def whole_kernel(ring, origins, psf_ref, shifts_ref, pieces_ref, *outs):
     slots, paired = pieces_ref.shape[1:3]
-    high, low = split(banded(order, masks, False, paired // 2, slots, psf_ref, shifts_ref))
+    parts = parts_of(banded(ring, origins, paired // 2, slots, psf_ref, shifts_ref))
     epoch = lax.axis_index("epoch")
     shifts = [shifts_ref[0, epoch * slots + e] for e in range(slots)]
-    store_blocks(product_of([pieces_ref], shifts, high, low), outs)
+    store_blocks(product_of(parts, [pieces_ref], shifts), outs)
 
 
 def grant(bytes_used):
     return pltpu.CompilerParams(vmem_limit_bytes=min(4 * bytes_used, 60 << 20))
 
 
-def exchange(array, axis, mask):
-    count = lax.axis_size(axis)
-    return lax.ppermute(array, axis, [(i, i ^ mask) for i in range(count)])
+def send(array, axis, targets):
+    return lax.ppermute(array, axis, list(enumerate(targets)))
+
+
+def target_of(ring, step, device):
+    return ring[(ring.index(device) + step) % len(ring)]
+
+
+def rotate(array, axis, ring, step):
+    return lax.ppermute(array, axis, [(i, target_of(ring, step, i)) for i in ring])
 
 
 def per_device(science, variance, psf, shifts):
     slots, height, breadth = science.shape
     order = lax.axis_size("epoch")
     sources = lax.axis_size("vel")
+    ring = RING if order == len(RING) else tuple(range(order))
     paired = 2 * height
     shifts = shifts.reshape(shifts.shape[:2])
     filtered = pl.pallas_call(
@@ -195,51 +219,51 @@
     depth = sources * slots * paired
     used = grant(4 * (sources * filtered.size + 2 * rows_all * (depth + breadth)))
     chunk = jax.ShapeDtypeStruct((2, block, breadth), jnp.float32)
-    if sources == 8:
-        across = exchange(filtered, "vel", 6)
-        along = exchange(filtered, "vel", 4)
-        aside = exchange(filtered, "vel", 2)
-        own = jnp.stack([filtered, across, along, aside])
-        twin = exchange(own, "vel", 1)
-        masks = [0, 6, 4, 2, 1, 7, 5, 3]
-        state = pl.pallas_call(
-            functools.partial(matrix_kernel, order, masks, height),
-            out_shape=[
-                jax.ShapeDtypeStruct((2 * rows_all, depth), jnp.bfloat16),
-                jax.ShapeDtypeStruct((2 * rows_all, depth), jnp.bfloat16),
-                jax.ShapeDtypeStruct((slots, 8, LANES), jnp.int32),
-            ],
+    if sources == 2 * len(ROUNDS[0]):
+        rounds = [[2 * t + c for t in targets for c in range(2)] for targets in ROUNDS]
+        arrived = [send(filtered, "vel", targets) for targets in rounds]
+        own = jnp.stack([filtered] + arrived[:-1])
+        last = arrived[-1][None]
+        sibling = [v ^ 1 for v in range(sources)]
+        twin = send(own, "vel", sibling)
+        twin_last = send(last, "vel", sibling)
+        origins = [list(range(sources))] + [[t.index(v) for v in range(sources)] for t in rounds]
+        origins = origins + [[row[v ^ 1] for v in range(sources)] for row in origins]
+        groups = [[own, last], [twin], [twin_last]]
+        depths = [sum(p.shape[0] for p in g) * slots * paired for g in groups]
+        column, *parts = pl.pallas_call(
+            functools.partial(matrix_kernel, ring, origins, height),
+            out_shape=[jax.ShapeDtypeStruct((slots, 8, LANES), jnp.int32)]
+            + [jax.ShapeDtypeStruct((2 * rows_all, 3 * d), jnp.bfloat16) for d in depths],
             in_specs=[SMEM] * 2,
-            out_specs=[VMEM] * 3,
+            out_specs=[VMEM] * (1 + len(depths)),
             compiler_params=used,
             name="matrix",
         )(psf, shifts)
-        partial = pl.pallas_call(
-            early_kernel,
-            out_shape=jax.ShapeDtypeStruct((2 * rows_all, breadth), jnp.float32),
-            in_specs=[VMEM] * 4,
-            out_specs=VMEM,
-            compiler_params=used,
-            name="early",
-        )(*state, own)
-        chunks = pl.pallas_call(
-            late_kernel,
-            out_shape=[chunk] * order,
-            in_specs=[VMEM] * 5,
-            out_specs=[VMEM] * order,
-            compiler_params=used,
-            name="late",
-        )(*state, partial, twin)
+        partial = []
+        for name, group, left in zip(("early", "middle", "late"), groups, parts):
+            shapes = [jax.ShapeDtypeStruct((2 * rows_all, breadth), jnp.float32)]
+            if name == "late":
+                shapes = [chunk] * order
+            operands = [column, left, *group, *partial]
+            partial = pl.pallas_call(
+                functools.partial(stack_kernel, len(group), bool(partial)),
+                out_shape=shapes,
+                in_specs=[VMEM] * len(operands),
+                out_specs=[VMEM] * len(shapes),
+                compiler_params=used,
+            )(*operands)
+        chunks = partial
     else:
         chunks = pl.pallas_call(
-            functools.partial(whole_kernel, order, list(range(sources))),
+            functools.partial(whole_kernel, ring, [[s] * sources for s in range(sources)]),
             out_shape=[chunk] * order,
             in_specs=[SMEM] * 2 + [VMEM],
             out_specs=[VMEM] * order,
             compiler_params=used,
             name="stack",
         )(psf, shifts, lax.all_gather(filtered, "vel"))
-    terms = [chunks[0]] + [exchange(chunks[k], "epoch", k) for k in range(1, order)]
+    terms = [chunks[0]] + [rotate(chunks[k], "epoch", ring, k) for k in range(1, order)]
     psi, phi = (sum(t[m] for t in terms) for m in range(2))
     return (psi / jnp.sqrt(phi))[None]
 

time: 24.2 us -> 26.8 us (1.11)
  starting transfers between devices: 9.1 us -> 10.3 us
  waiting for transfers between devices: 11.1 us -> 12.2 us
    ppermute x7 -> x8, starting transfers between devices: 9.1 us -> 10.3 us  [the longest x3 5.68 us: rotate(): lax.ppermute(array, axis, [(i, target_of(ring, step, i)) for i in ring])]
    ppermute x7 -> x8, waiting for transfers between devices: 11.1 us -> 12.2 us  [the longest x5 9.09 us: send(): return lax.ppermute(array, axis, list(enumerate(targets)))]
    pallas_call x3 -> x4, Pallas kernels: 1.42 us -> 1.66 us  [the longest x3 0.91 us: per_device(): pl.pallas_call(functools.partial(stack_kernel, len(group), bool(partial))...]
  transfers between devices with their start and end apart: 7 -> 8, of which waited for: 5 -> 5; matrix products, arithmetic and copies ran while one was open for 0% -> 0% of each run, Pallas kernels for 4% -> 5%
where the time goes in v3:
time: 26.8 us; the launch traced here: 26.7 us
  waiting for transfers between devices  12.2 us (46%)
  starting transfers between devices  10.3 us (38%)
  Pallas kernels  2.72 us (10%)
  local copies, waits for them, and re-layouts  0.69 us (3%)
  other arithmetic  0.65 us (2%)
    ppermute x5, waiting for transfers between devices, send(): return lax.ppermute(array, axis, list(enumerate(targets)))  9.09 us
    ppermute x3, starting transfers between devices, rotate(): lax.ppermute(array, axis, [(i, target_of(ring, step, i)) for i in ring])  5.68 us
    ppermute x5, starting transfers between devices, send(): return lax.ppermute(array, axis, list(enumerate(targets)))  4.62 us
    ppermute x3, waiting for transfers between devices, rotate(): lax.ppermute(array, axis, [(i, target_of(ring, step, i)) for i in ring])  3.13 us
    pallas_call x1, Pallas kernels, per_device(): pl.pallas_call(columns_kernel, out_shape=jax.ShapeDtypeStruct((slots, pai...  1.06 us
    pallas_call x3, Pallas kernels, per_device(): pl.pallas_call(functools.partial(stack_kernel, len(group), bool(partial))...  0.91 us
    pallas_call x1, Pallas kernels, per_device(): pl.pallas_call(functools.partial(matrix_kernel, ring, origins, height), o...  0.75 us
    unnamed x4, local copies, waits for them, and re-layouts  0.69 us
  transfers between devices with their start and end apart: 8, of which 5 were waited for; matrix products, arithmetic and copies ran while one was open for 0% of the time, Pallas kernels for 5%

profile of v3, /device:TPU:0, one launch (start us, length us, event | category | flops | bytes accessed | tf_op | source)
XLA Modules:
  0.0 26.7 jit_solution(9676252655271929493)
XLA Ops:
  0.0 1.1 %columns.1 = f32[2,8,1024]{2,1,0:T(8,128)S(1)} custom-call(f32[2,4,1024]{2,1,0:T(4,128)} %science_hbm.1, f32[2,4,1024]{2,1,0:T(4,128)} %variance_hbm.1, f32[2,9]{1,0:T(2,128)} %psf_hbm.1), custom_call_target="tpu_custom_call" | custom-call | tf_op jit(solution)/shard_map/columns/pallas_call | solution.py:203
  1.1 4.0 %collective-permute-start.3 = (f32[2,8,1024]{2,1,0:T(8,128)S(1)}, f32[2,8,1024]{2,1,0:T(8,128)S(1)}, u32[]{:S(2)}, u32[]{:S(2)}) collective-permute-start(f32[2,8,1024]{2,1,0:T(8,128)S(1)} %columns.1), channel_id=1, source_target_pairs={{0,6},{1,7},{2,0},{3,1},{4,2},{5,3},{6,4},{7,5},{8,14},{9,15},{10,... | collective-permute-start | bytes 196616 | tf_op jit(solution)/shard_map/ppermute | solution.py:185
  5.0 0.0 collective-permute-start.2
  5.0 2.0 %collective-permute-done.3 = f32[2,8,1024]{2,1,0:T(8,128)S(1)} collective-permute-done((f32[2,8,1024]{2,1,0:T(8,128)S(1)}, f32[2,8,1024]{2,1,0:T(8,128)S(1)}, u32[]{:S(2)}, u32[]{:S(2)}) %collective-permute-start.3) | collective-permute-done | bytes 65568 | tf_op jit(solution)/shard_map/ppermute | solution.py:185
  7.1 3.1 %collective-permute-done.2 = f32[2,8,1024]{2,1,0:T(8,128)S(1)} collective-permute-done((f32[2,8,1024]{2,1,0:T(8,128)S(1)}, f32[2,8,1024]{2,1,0:T(8,128)S(1)}, u32[]{:S(2)}, u32[]{:S(2)}) %collective-permute-start.2) | collective-permute-done | bytes 65568 | tf_op jit(solution)/shard_map/ppermute | solution.py:185
  10.2 0.1 collective-permute-start.4
  10.3 0.6 %collective-permute-start = (f32[2,8,1024]{2,1,0:T(8,128)S(1)}, f32[2,8,1024]{2,1,0:T(8,128)S(1)}, u32[]{:S(2)}, u32[]{:S(2)}) collective-permute-start(f32[2,8,1024]{2,1,0:T(8,128)S(1)} %columns.1), channel_id=1, source_target_pairs={{0,4},{1,5},{2,6},{3,7},{4,0},{5,1},{6,2},{7,3},{8,12},{9,13},{10,... | collective-permute-start | bytes 196616 | tf_op jit(solution)/shard_map/ppermute | solution.py:185
  10.9 3.9 %collective-permute-done = f32[2,8,1024]{2,1,0:T(8,128)S(1)} collective-permute-done((f32[2,8,1024]{2,1,0:T(8,128)S(1)}, f32[2,8,1024]{2,1,0:T(8,128)S(1)}, u32[]{:S(2)}, u32[]{:S(2)}) %collective-permute-start) | collective-permute-done | bytes 65568 | tf_op jit(solution)/shard_map/ppermute | solution.py:185
  14.8 0.0 copy-start.1
  14.8 0.0 copy-start
  14.8 0.0 collective-permute-start.1
  14.8 0.7 %copy-done.1 = s32[2,8,1]{1,2,0:T(1,128)S(1)} copy-done((s32[2,8,1]{1,2,0:T(1,128)S(1)}, s32[2,8,1]{1,2,0:T(1,128)}, u32[]{:S(2)}) %copy-start.1) | copy-done | bytes 88
  15.5 0.0 copy-done
  15.5 0.7 %matrix.1 = (s32[2,8,128]{2,1,0:T(8,128)S(1)}, bf16[64,192]{1,0:T(8,128)(2,1)S(1)}, bf16[64,144]{1,0:T(8,128)(2,1)S(1)}, bf16[64,48]{1,0:T(8,128)(2,1)S(1)}) custom-call(f32[2,9]{1,0:T(2,128)S(1)} %copy-done, s32[2,8]{1,0:T(2,128)S(1)} %bitcast.8), custom_call_target="tpu_custom_call" | custom-call | tf_op jit(solution)/shard_map/matrix/pallas_call | solution.py:234
  16.2 0.3 %shard_map.46.refs_1_ = f32[64,1024]{1,0:T(8,128)S(1)} custom-call(s32[2,8,128]{2,1,0:T(8,128)S(1)} %get-tuple-element.13.column_ref, bf16[64,192]{1,0:T(8,128)(2,1)S(1)} %get-tuple-element.16.parts_ref, f32[3,2,8,1024]{3,2,1,0:T(8,128)S(1)} %pad_maximum_fusion.refs_0_, f32[1,2,8,1024]{3,2,1,0:T(8,128)S(1)} %bitcast.7), custom_call_target="tpu_custom_call" | custom-call | tf_op jit(solution)/shard_map/pallas_call | solution.py:249
  16.6 0.0 collective-permute-done.4.refs_0_
  16.6 0.3 %shard_map.47.refs_1_ = f32[64,1024]{1,0:T(8,128)S(1)} custom-call(s32[2,8,128]{2,1,0:T(8,128)S(1)} %get-tuple-element.13.column_ref, bf16[64,144]{1,0:T(8,128)(2,1)S(1)} %get-tuple-element.15.parts_ref, f32[3,2,8,1024]{3,2,1,0:T(8,128)S(1)} %collective-permute-done.4.refs_0_, f32[64,1024]{1,0:T(8,128)S(1)} %shard_map.46.refs_1_), custom_call_target="tpu_custom_call" | custom-call | tf_op jit(solution)/shard_map/pallas_call | solution.py:249
  16.9 0.0 collective-permute-done.1.refs_0_
  16.9 0.3 %shard_map.48 = (f32[2,8,1024]{2,1,0:T(8,128)S(1)}, f32[2,8,1024]{2,1,0:T(8,128)S(1)}, f32[2,8,1024]{2,1,0:T(8,128)S(1)}, f32[2,8,1024]{2,1,0:T(8,128)S(1)}) custom-call(s32[2,8,128]{2,1,0:T(8,128)S(1)} %get-tuple-element.13.column_ref, bf16[64,48]{1,0:T(8,128)(2,1)S(1)} %get-tuple-element.14.parts_ref, ...), custom_call_target="tpu_custom_call" | custom-call | tf_op jit(solution)/shard_map/pallas_call | solution.py:249
  17.2 1.6 %collective-permute-start.5 = (f32[2,8,1024]{2,1,0:T(8,128)S(1)}, f32[2,8,1024]{2,1,0:T(8,128)S(1)}, u32[]{:S(2)}, u32[]{:S(2)}) collective-permute-start(f32[2,8,1024]{2,1,0:T(8,128)S(1)} %get-tuple-element.18), channel_id=1, source_target_pairs={{0,8},{8,24},{24,16},{16,0},{1,9},{9,25},{25,17},{17,1},{2,10},{10... | collective-permute-start | bytes 196616 | tf_op jit(solution)/shard_map/ppermute | solution.py:193
  18.8 2.5 %collective-permute-start.6 = (f32[2,8,1024]{2,1,0:T(8,128)S(1)}, f32[2,8,1024]{2,1,0:T(8,128)S(1)}, u32[]{:S(2)}, u32[]{:S(2)}) collective-permute-start(f32[2,8,1024]{2,1,0:T(8,128)S(1)} %get-tuple-element.19), channel_id=1, source_target_pairs={{0,24},{8,16},{24,0},{16,8},{1,25},{9,17},{25,1},{17,9},{2,26},{10... | collective-permute-start | bytes 196616 | tf_op jit(solution)/shard_map/ppermute | solution.py:193
  21.3 1.6 %collective-permute-start.7 = (f32[2,8,1024]{2,1,0:T(8,128)S(1)}, f32[2,8,1024]{2,1,0:T(8,128)S(1)}, u32[]{:S(2)}, u32[]{:S(2)}) collective-permute-start(f32[2,8,1024]{2,1,0:T(8,128)S(1)} %get-tuple-element.20), channel_id=1, source_target_pairs={{0,16},{8,0},{24,8},{16,24},{1,17},{9,1},{25,9},{17,25},{2,18},{10... | collective-permute-start | bytes 196616 | tf_op jit(solution)/shard_map/ppermute | solution.py:193
  22.9 0.0 collective-permute-done.5
  22.9 2.9 %collective-permute-done.6 = f32[2,8,1024]{2,1,0:T(8,128)S(1)} collective-permute-done((f32[2,8,1024]{2,1,0:T(8,128)S(1)}, f32[2,8,1024]{2,1,0:T(8,128)S(1)}, u32[]{:S(2)}, u32[]{:S(2)}) %collective-permute-start.6) | collective-permute-done | bytes 65568 | tf_op jit(solution)/shard_map/ppermute | solution.py:193
  25.8 0.2 collective-permute-done.7
  26.0 0.6 %fusion.1 = f32[1,8,1024]{2,1,0:T(8,128)} fusion(f32[2,8,1024]{2,1,0:T(8,128)S(1)} %collective-permute-done.7, f32[2,8,1024]{2,1,0:T(8,128)S(1)} %collective-permute-done.6, f32[2,8,1024]{2,1,0:T(8,128)S(1)} %collective-permute-done.5, f32[2,8,1024]{2,1,0:T(8,128)S(1)} %get-tuple-element.17), kind=kLoop, calls=%fused_computation.3 | loop fusion | flops 57344 | bytes 294912 | tf_op jit(solution)/shard_map/div | solution.py:268
  (1 shorter events, 0.0 us)
Async XLA Ops:
  1.1 6.0 %collective-permute-start.3 = (f32[2,8,1024]{2,1,0:T(8,128)S(1)}, f32[2,8,1024]{2,1,0:T(8,128)S(1)}, u32[]{:S(2)}, u32[]{:S(2)}) collective-permute-start(f32[2,8,1024]{2,1,0:T(8,128)S(1)} %columns.1), channel_id=1, source_target_pairs={{0,6},{1,7},{2,0},{3,1},{4,2},{5,3},{6,4},{7,5},{8,14},{9,15},{10,... | collective-permute-start | bytes 196616 | tf_op jit(solution)/shard_map/ppermute | solution.py:185
  5.0 5.2 %collective-permute-start.2 = (f32[2,8,1024]{2,1,0:T(8,128)S(1)}, f32[2,8,1024]{2,1,0:T(8,128)S(1)}, u32[]{:S(2)}, u32[]{:S(2)}) collective-permute-start(f32[2,8,1024]{2,1,0:T(8,128)S(1)} %columns.1), channel_id=1, source_target_pairs={{0,2},{1,3},{2,4},{3,5},{4,6},{5,7},{6,0},{7,1},{8,10},{9,11},{10,... | collective-permute-start | bytes 196616 | tf_op jit(solution)/shard_map/ppermute | solution.py:185
  10.2 6.4 %collective-permute-start.4 = (f32[3,2,8,1024]{3,2,1,0:T(8,128)S(1)}, f32[3,2,8,1024]{3,2,1,0:T(8,128)S(1)}, u32[]{:S(2)}, u32[]{:S(2)}) collective-permute-start(f32[3,2,8,1024]{3,2,1,0:T(8,128)S(1)} %pad_maximum_fusion.refs_0_), channel_id=1, source_target_pairs={{0,1},{1,0},{2,3},{3,2},{4,5},{5,4},{6,7},{7,6},{8,9},{9,8},{10,11... | collective-permute-start | bytes 589832 | tf_op jit(solution)/shard_map/ppermute | solution.py:185
  10.3 4.5 %collective-permute-start = (f32[2,8,1024]{2,1,0:T(8,128)S(1)}, f32[2,8,1024]{2,1,0:T(8,128)S(1)}, u32[]{:S(2)}, u32[]{:S(2)}) collective-permute-start(f32[2,8,1024]{2,1,0:T(8,128)S(1)} %columns.1), channel_id=1, source_target_pairs={{0,4},{1,5},{2,6},{3,7},{4,0},{5,1},{6,2},{7,3},{8,12},{9,13},{10,... | collective-permute-start | bytes 196616 | tf_op jit(solution)/shard_map/ppermute | solution.py:185
  14.8 0.7 %copy-start.1 = (s32[2,8,1]{1,2,0:T(1,128)S(1)}, s32[2,8,1]{1,2,0:T(1,128)}, u32[]{:S(2)}) copy-start(s32[2,8,1]{1,2,0:T(1,128)} %param.7) | copy-start | bytes 196
  14.8 0.7 %copy-start = (f32[2,9]{1,0:T(2,128)S(1)}, f32[2,9]{1,0:T(2,128)}, u32[]{:S(2)}) copy-start(f32[2,9]{1,0:T(2,128)} %psf_hbm.1) | copy-start | bytes 220
  14.8 2.1 %collective-permute-start.1 = (f32[1,2,8,1024]{3,2,1,0:T(8,128)S(1)}, f32[1,2,8,1024]{3,2,1,0:T(8,128)S(1)}, u32[]{:S(2)}, u32[]{:S(2)}) collective-permute-start(f32[1,2,8,1024]{3,2,1,0:T(8,128)S(1)} %bitcast.6), channel_id=1, source_target_pairs={{0,1},{1,0},{2,3},{3,2},{4,5},{5,4},{6,7},{7,6},{8,9},{9,8},{10,11... | collective-permute-start | bytes 196616 | tf_op jit(solution)/shard_map/ppermute | solution.py:185
  17.2 5.7 %collective-permute-start.5 = (f32[2,8,1024]{2,1,0:T(8,128)S(1)}, f32[2,8,1024]{2,1,0:T(8,128)S(1)}, u32[]{:S(2)}, u32[]{:S(2)}) collective-permute-start(f32[2,8,1024]{2,1,0:T(8,128)S(1)} %get-tuple-element.18), channel_id=1, source_target_pairs={{0,8},{8,24},{24,16},{16,0},{1,9},{9,25},{25,17},{17,1},{2,10},{10... | collective-permute-start | bytes 196616 | tf_op jit(solution)/shard_map/ppermute | solution.py:193
  18.8 6.9 %collective-permute-start.6 = (f32[2,8,1024]{2,1,0:T(8,128)S(1)}, f32[2,8,1024]{2,1,0:T(8,128)S(1)}, u32[]{:S(2)}, u32[]{:S(2)}) collective-permute-start(f32[2,8,1024]{2,1,0:T(8,128)S(1)} %get-tuple-element.19), channel_id=1, source_target_pairs={{0,24},{8,16},{24,0},{16,8},{1,25},{9,17},{25,1},{17,9},{2,26},{10... | collective-permute-start | bytes 196616 | tf_op jit(solution)/shard_map/ppermute | solution.py:193
  21.3 4.7 %collective-permute-start.7 = (f32[2,8,1024]{2,1,0:T(8,128)S(1)}, f32[2,8,1024]{2,1,0:T(8,128)S(1)}, u32[]{:S(2)}, u32[]{:S(2)}) collective-permute-start(f32[2,8,1024]{2,1,0:T(8,128)S(1)} %get-tuple-element.20), channel_id=1, source_target_pairs={{0,16},{8,0},{24,8},{16,24},{1,17},{9,1},{25,9},{17,25},{2,18},{10... | collective-permute-start | bytes 196616 | tf_op jit(solution)/shard_map/ppermute | solution.py:193

commit v4 on v3

--- a/solution.py
+++ b/solution.py
@@ -13,7 +13,7 @@
 HBM = pl.BlockSpec(memory_space=pltpu.HBM)
 LANES = 128
 ROUNDS = ((1, 2, 3, 0), (3, 0, 1, 2), (2, 3, 0, 1))
-RING = (0, 1, 3, 2)
+STEPS = ((1, 2, 0, 3), (2, 3, 1, 0), (3, 0, 2, 1), (0, 1, 3, 2))
 
 
 def tiles_of(x):
@@ -62,13 +62,13 @@
     return sum(jnp.where(index == i, jnp.int32(v), 0) for i, v in enumerate(values))
 
 
-def banded(ring, origins, height, slots, psf_ref, shifts_ref):
+def banded(steps, origins, height, slots, psf_ref, shifts_ref):
     taps = psf_ref.shape[1]
     radius = taps // 2
     sources = len(origins)
     paired = 2 * height
     rows_all = sources * height
-    order = len(ring)
+    order = len(steps)
     block = rows_all // order
     depth = sources * slots * paired
     epoch = lax.axis_index("epoch")
@@ -78,7 +78,7 @@
     out_member = (out_at // block) % 2
     out_block = jnp.zeros_like(step)
     for k in range(order):
-        target = chosen([target_of(ring, k, i) for i in range(order)], epoch)
+        target = chosen(steps[k], epoch)
         out_block = jnp.where(step == k, target, out_block)
     out_row = out_block * block + out_at % block
     in_at = lax.broadcasted_iota(jnp.int32, (1, depth), 1)
@@ -143,9 +143,9 @@
             at += rows
 
 
-def matrix_kernel(ring, origins, height, psf_ref, shifts_ref, column_ref, *parts_refs):
+def matrix_kernel(steps, origins, height, psf_ref, shifts_ref, column_ref, *parts_refs):
     slots = column_ref.shape[0]
-    matrix = banded(ring, origins, height, slots, psf_ref, shifts_ref)
+    matrix = banded(steps, origins, height, slots, psf_ref, shifts_ref)
     at = 0
     for ref in parts_refs:
         depth = ref.shape[1] // 3
@@ -169,9 +169,9 @@
         store_blocks(product, refs)
 
 
-def whole_kernel(ring, origins, psf_ref, shifts_ref, pieces_ref, *outs):
+def whole_kernel(steps, origins, psf_ref, shifts_ref, pieces_ref, *outs):
     slots, paired = pieces_ref.shape[1:3]
-    parts = parts_of(banded(ring, origins, paired // 2, slots, psf_ref, shifts_ref))
+    parts = parts_of(banded(steps, origins, paired // 2, slots, psf_ref, shifts_ref))
     epoch = lax.axis_index("epoch")
     shifts = [shifts_ref[0, epoch * slots + e] for e in range(slots)]
     store_blocks(product_of(parts, [pieces_ref], shifts), outs)
@@ -185,19 +185,21 @@
     return lax.ppermute(array, axis, list(enumerate(targets)))
 
 
-def target_of(ring, step, device):
-    return ring[(ring.index(device) + step) % len(ring)]
-
-
-def rotate(array, axis, ring, step):
-    return lax.ppermute(array, axis, [(i, target_of(ring, step, i)) for i in ring])
+def hand(array, targets, grid):
+    pairs = []
+    for i, t in enumerate(targets):
+        for v in range(grid):
+            pairs.append((i * grid + v, t * grid + (v ^ 1 if t == i else v)))
+    return lax.ppermute(array, ("epoch", "vel"), pairs)
 
 
 def per_device(science, variance, psf, shifts):
     slots, height, breadth = science.shape
     order = lax.axis_size("epoch")
     sources = lax.axis_size("vel")
-    ring = RING if order == len(RING) else tuple(range(order))
+    steps = STEPS
+    if order != len(STEPS):
+        steps = [[(i + k) % order for i in range(order)] for k in range(order)]
     paired = 2 * height
     shifts = shifts.reshape(shifts.shape[:2])
     filtered = pl.pallas_call(
@@ -232,7 +234,7 @@
         groups = [[own, last], [twin], [twin_last]]
         depths = [sum(p.shape[0] for p in g) * slots * paired for g in groups]
         column, *parts = pl.pallas_call(
-            functools.partial(matrix_kernel, ring, origins, height),
+            functools.partial(matrix_kernel, steps, origins, height),
             out_shape=[jax.ShapeDtypeStruct((slots, 8, LANES), jnp.int32)]
             + [jax.ShapeDtypeStruct((2 * rows_all, 3 * d), jnp.bfloat16) for d in depths],
             in_specs=[SMEM] * 2,
@@ -256,14 +258,18 @@
         chunks = partial
     else:
         chunks = pl.pallas_call(
-            functools.partial(whole_kernel, ring, [[s] * sources for s in range(sources)]),
+            functools.partial(whole_kernel, steps, [[s] * sources for s in range(sources)]),
             out_shape=[chunk] * order,
             in_specs=[SMEM] * 2 + [VMEM],
             out_specs=[VMEM] * order,
             compiler_params=used,
             name="stack",
         )(psf, shifts, lax.all_gather(filtered, "vel"))
-    terms = [chunks[0]] + [rotate(chunks[k], "epoch", ring, k) for k in range(1, order)]
+    terms = []
+    for k, targets in enumerate(steps):
+        came = hand(chunks[k], targets, sources)
+        kept = chosen([int(t == i) for i, t in enumerate(targets)], lax.axis_index("epoch"))
+        terms.append(jnp.where(kept == 1, chunks[k], came))
     psi, phi = (sum(t[m] for t in terms) for m in range(2))
     return (psi / jnp.sqrt(phi))[None]
 

time: 26.8 us -> 26.7 us (level)
  waiting for transfers between devices: 12.2 us -> 10.9 us
  starting transfers between devices: 10.3 us -> 11.4 us
    ppermute x5, waiting for transfers between devices: 9.09 us -> 7.03 us  [send(): return lax.ppermute(array, axis, list(enumerate(targets)))]
    ppermute x3 -> x4, waiting for transfers between devices: 3.13 us -> 3.86 us  [hand(): return lax.ppermute(array, ('epoch', 'vel'), pairs)]
    ppermute x5, starting transfers between devices: 4.62 us -> 5.26 us  [send(): return lax.ppermute(array, axis, list(enumerate(targets)))]
    ppermute x3 -> x4, starting transfers between devices: 5.68 us -> 6.13 us  [hand(): return lax.ppermute(array, ('epoch', 'vel'), pairs)]
  transfers between devices with their start and end apart: 8 -> 9, of which waited for: 5 -> 4; matrix products, arithmetic and copies ran while one was open for 0% -> 0% of each run, Pallas kernels for 5% -> 5%
where the time goes in v4:
time: 26.7 us; the launch traced here: 26.5 us
  starting transfers between devices  11.4 us (43%)
  waiting for transfers between devices  10.9 us (41%)
  Pallas kernels  2.72 us (10%)
  local copies, waits for them, and re-layouts  0.69 us (3%)
  other arithmetic  0.68 us (3%)
    ppermute x5, waiting for transfers between devices, send(): return lax.ppermute(array, axis, list(enumerate(targets)))  7.03 us
    ppermute x4, starting transfers between devices, hand(): return lax.ppermute(array, ('epoch', 'vel'), pairs)  6.13 us
    ppermute x5, starting transfers between devices, send(): return lax.ppermute(array, axis, list(enumerate(targets)))  5.26 us
    ppermute x4, waiting for transfers between devices, hand(): return lax.ppermute(array, ('epoch', 'vel'), pairs)  3.86 us
    pallas_call x1, Pallas kernels, per_device(): pl.pallas_call(columns_kernel, out_shape=jax.ShapeDtypeStruct((slots, pai...  1.06 us
    pallas_call x3, Pallas kernels, per_device(): pl.pallas_call(functools.partial(stack_kernel, len(group), bool(partial))...  0.91 us
    pallas_call x1, Pallas kernels, per_device(): pl.pallas_call(functools.partial(matrix_kernel, steps, origins, height),...  0.75 us
    unnamed x4, local copies, waits for them, and re-layouts  0.69 us
  transfers between devices with their start and end apart: 9, of which 4 were waited for; matrix products, arithmetic and copies ran while one was open for 0% of the time, Pallas kernels for 5%

profile of v4, /device:TPU:0, one launch (start us, length us, event | category | flops | bytes accessed | tf_op | source)
XLA Modules:
  0.0 26.5 jit_solution(6685445685444962630)
XLA Ops:
  0.0 1.1 %columns.1 = f32[2,8,1024]{2,1,0:T(8,128)S(1)} custom-call(f32[2,4,1024]{2,1,0:T(4,128)} %science_hbm.1, f32[2,4,1024]{2,1,0:T(4,128)} %variance_hbm.1, f32[2,9]{1,0:T(2,128)} %psf_hbm.1), custom_call_target="tpu_custom_call" | custom-call | tf_op jit(solution)/shard_map/columns/pallas_call | solution.py:205
  1.1 3.0 %collective-permute-start.2 = (f32[2,8,1024]{2,1,0:T(8,128)S(1)}, f32[2,8,1024]{2,1,0:T(8,128)S(1)}, u32[]{:S(2)}, u32[]{:S(2)}) collective-permute-start(f32[2,8,1024]{2,1,0:T(8,128)S(1)} %columns.1), channel_id=1, source_target_pairs={{0,2},{1,3},{2,4},{3,5},{4,6},{5,7},{6,0},{7,1},{8,10},{9,11},{10,... | collective-permute-start | bytes 196616 | tf_op jit(solution)/shard_map/ppermute | solution.py:185
  4.1 1.0 %collective-permute-start.3 = (f32[2,8,1024]{2,1,0:T(8,128)S(1)}, f32[2,8,1024]{2,1,0:T(8,128)S(1)}, u32[]{:S(2)}, u32[]{:S(2)}) collective-permute-start(f32[2,8,1024]{2,1,0:T(8,128)S(1)} %columns.1), channel_id=1, source_target_pairs={{0,6},{1,7},{2,0},{3,1},{4,2},{5,3},{6,4},{7,5},{8,14},{9,15},{10,... | collective-permute-start | bytes 196616 | tf_op jit(solution)/shard_map/ppermute | solution.py:185
  5.1 2.3 %collective-permute-done.2 = f32[2,8,1024]{2,1,0:T(8,128)S(1)} collective-permute-done((f32[2,8,1024]{2,1,0:T(8,128)S(1)}, f32[2,8,1024]{2,1,0:T(8,128)S(1)}, u32[]{:S(2)}, u32[]{:S(2)}) %collective-permute-start.2) | collective-permute-done | bytes 65568 | tf_op jit(solution)/shard_map/ppermute | solution.py:185
  7.4 1.4 %collective-permute-done.3 = f32[2,8,1024]{2,1,0:T(8,128)S(1)} collective-permute-done((f32[2,8,1024]{2,1,0:T(8,128)S(1)}, f32[2,8,1024]{2,1,0:T(8,128)S(1)}, u32[]{:S(2)}, u32[]{:S(2)}) %collective-permute-start.3) | collective-permute-done | bytes 65568 | tf_op jit(solution)/shard_map/ppermute | solution.py:185
  8.8 0.1 collective-permute-start.4
  8.9 1.1 %collective-permute-start = (f32[2,8,1024]{2,1,0:T(8,128)S(1)}, f32[2,8,1024]{2,1,0:T(8,128)S(1)}, u32[]{:S(2)}, u32[]{:S(2)}) collective-permute-start(f32[2,8,1024]{2,1,0:T(8,128)S(1)} %columns.1), channel_id=1, source_target_pairs={{0,4},{1,5},{2,6},{3,7},{4,0},{5,1},{6,2},{7,3},{8,12},{9,13},{10,... | collective-permute-start | bytes 196616 | tf_op jit(solution)/shard_map/ppermute | solution.py:185
  10.0 3.3 %collective-permute-done = f32[2,8,1024]{2,1,0:T(8,128)S(1)} collective-permute-done((f32[2,8,1024]{2,1,0:T(8,128)S(1)}, f32[2,8,1024]{2,1,0:T(8,128)S(1)}, u32[]{:S(2)}, u32[]{:S(2)}) %collective-permute-start) | collective-permute-done | bytes 65568 | tf_op jit(solution)/shard_map/ppermute | solution.py:185
  13.4 0.0 copy-start.1
  13.4 0.0 copy-start
  13.4 0.0 collective-permute-start.1
  13.4 0.7 %copy-done.1 = s32[2,8,1]{1,2,0:T(1,128)S(1)} copy-done((s32[2,8,1]{1,2,0:T(1,128)S(1)}, s32[2,8,1]{1,2,0:T(1,128)}, u32[]{:S(2)}) %copy-start.1) | copy-done | bytes 88
  14.1 0.0 copy-done
  14.1 0.7 %matrix.1 = (s32[2,8,128]{2,1,0:T(8,128)S(1)}, bf16[64,192]{1,0:T(8,128)(2,1)S(1)}, bf16[64,144]{1,0:T(8,128)(2,1)S(1)}, bf16[64,48]{1,0:T(8,128)(2,1)S(1)}) custom-call(f32[2,9]{1,0:T(2,128)S(1)} %copy-done, s32[2,8]{1,0:T(2,128)S(1)} %bitcast.8), custom_call_target="tpu_custom_call" | custom-call | tf_op jit(solution)/shard_map/matrix/pallas_call | solution.py:236
  14.8 0.3 %shard_map.46.refs_1_ = f32[64,1024]{1,0:T(8,128)S(1)} custom-call(s32[2,8,128]{2,1,0:T(8,128)S(1)} %get-tuple-element.13.column_ref, bf16[64,192]{1,0:T(8,128)(2,1)S(1)} %get-tuple-element.16.parts_ref, f32[3,2,8,1024]{3,2,1,0:T(8,128)S(1)} %pad_maximum_fusion.refs_0_, f32[1,2,8,1024]{3,2,1,0:T(8,128)S(1)} %bitcast.7), custom_call_target="tpu_custom_call" | custom-call | tf_op jit(solution)/shard_map/pallas_call | solution.py:251
  15.2 0.0 collective-permute-done.4.refs_0_
  15.2 0.3 %shard_map.47.refs_1_ = f32[64,1024]{1,0:T(8,128)S(1)} custom-call(s32[2,8,128]{2,1,0:T(8,128)S(1)} %get-tuple-element.13.column_ref, bf16[64,144]{1,0:T(8,128)(2,1)S(1)} %get-tuple-element.15.parts_ref, f32[3,2,8,1024]{3,2,1,0:T(8,128)S(1)} %collective-permute-done.4.refs_0_, f32[64,1024]{1,0:T(8,128)S(1)} %shard_map.46.refs_1_), custom_call_target="tpu_custom_call" | custom-call | tf_op jit(solution)/shard_map/pallas_call | solution.py:251
  15.5 0.0 collective-permute-done.1.refs_0_
  15.5 0.3 %shard_map.48 = (f32[2,8,1024]{2,1,0:T(8,128)S(1)}, f32[2,8,1024]{2,1,0:T(8,128)S(1)}, f32[2,8,1024]{2,1,0:T(8,128)S(1)}, f32[2,8,1024]{2,1,0:T(8,128)S(1)}) custom-call(s32[2,8,128]{2,1,0:T(8,128)S(1)} %get-tuple-element.13.column_ref, bf16[64,48]{1,0:T(8,128)(2,1)S(1)} %get-tuple-element.14.parts_ref, ...), custom_call_target="tpu_custom_call" | custom-call | tf_op jit(solution)/shard_map/pallas_call | solution.py:251
  15.8 1.6 %collective-permute-start.5 = (f32[2,8,1024]{2,1,0:T(8,128)S(1)}, f32[2,8,1024]{2,1,0:T(8,128)S(1)}, u32[]{:S(2)}, u32[]{:S(2)}) collective-permute-start(f32[2,8,1024]{2,1,0:T(8,128)S(1)} %get-tuple-element.17), channel_id=1, source_target_pairs={{0,8},{1,9},{2,10},{3,11},{4,12},{5,13},{6,14},{7,15},{8,16},{9,17... | collective-permute-start | bytes 196616 | tf_op jit(solution)/shard_map/ppermute | solution.py:193
  17.4 2.1 %collective-permute-start.7 = (f32[2,8,1024]{2,1,0:T(8,128)S(1)}, f32[2,8,1024]{2,1,0:T(8,128)S(1)}, u32[]{:S(2)}, u32[]{:S(2)}) collective-permute-start(f32[2,8,1024]{2,1,0:T(8,128)S(1)} %get-tuple-element.19), channel_id=1, source_target_pairs={{0,24},{1,25},{2,26},{3,27},{4,28},{5,29},{6,30},{7,31},{8,0},{9,1... | collective-permute-start | bytes 196616 | tf_op jit(solution)/shard_map/ppermute | solution.py:193
  19.5 0.1 collective-permute-start.8
  19.7 2.2 %collective-permute-start.6 = (f32[2,8,1024]{2,1,0:T(8,128)S(1)}, f32[2,8,1024]{2,1,0:T(8,128)S(1)}, u32[]{:S(2)}, u32[]{:S(2)}) collective-permute-start(f32[2,8,1024]{2,1,0:T(8,128)S(1)} %get-tuple-element.18), channel_id=1, source_target_pairs={{0,16},{1,17},{2,18},{3,19},{4,20},{5,21},{6,22},{7,23},{8,24},{9,... | collective-permute-start | bytes 196616 | tf_op jit(solution)/shard_map/ppermute | solution.py:193
  21.9 0.0 collective-permute-done.5
  21.9 0.0 collective-permute-done.7
  22.0 0.0 collective-permute-done.8
  22.0 3.8 %collective-permute-done.6 = f32[2,8,1024]{2,1,0:T(8,128)S(1)} collective-permute-done((f32[2,8,1024]{2,1,0:T(8,128)S(1)}, f32[2,8,1024]{2,1,0:T(8,128)S(1)}, u32[]{:S(2)}, u32[]{:S(2)}) %collective-permute-start.6) | collective-permute-done | bytes 65568 | tf_op jit(solution)/shard_map/ppermute | solution.py:193
  25.8 0.6 %fusion.1 = f32[1,8,1024]{2,1,0:T(8,128)} fusion(f32[2,8,1024]{2,1,0:T(8,128)S(1)} %broadcast_select_fusion, f32[2,8,1024]{2,1,0:T(8,128)S(1)} %broadcast_select_fusion.1, f32[2,8,1024]{2,1,0:T(8,128)S(1)} %collective-permute-done.6, f32[2,8,1024]{2,1,0:T(8,128)S(1)} %broadcast_select_fusion.2), kind=kLoop, calls=%fused_computation.3 | loop fusion | flops 57344 | bytes 294912 | tf_op jit(solution)/shard_map/div | solution.py:274
  (4 shorter events, 0.0 us)
Async XLA Ops:
  1.1 6.3 %collective-permute-start.2 = (f32[2,8,1024]{2,1,0:T(8,128)S(1)}, f32[2,8,1024]{2,1,0:T(8,128)S(1)}, u32[]{:S(2)}, u32[]{:S(2)}) collective-permute-start(f32[2,8,1024]{2,1,0:T(8,128)S(1)} %columns.1), channel_id=1, source_target_pairs={{0,2},{1,3},{2,4},{3,5},{4,6},{5,7},{6,0},{7,1},{8,10},{9,11},{10,... | collective-permute-start | bytes 196616 | tf_op jit(solution)/shard_map/ppermute | solution.py:185
  4.1 4.7 %collective-permute-start.3 = (f32[2,8,1024]{2,1,0:T(8,128)S(1)}, f32[2,8,1024]{2,1,0:T(8,128)S(1)}, u32[]{:S(2)}, u32[]{:S(2)}) collective-permute-start(f32[2,8,1024]{2,1,0:T(8,128)S(1)} %columns.1), channel_id=1, source_target_pairs={{0,6},{1,7},{2,0},{3,1},{4,2},{5,3},{6,4},{7,5},{8,14},{9,15},{10,... | collective-permute-start | bytes 196616 | tf_op jit(solution)/shard_map/ppermute | solution.py:185
  8.8 6.4 %collective-permute-start.4 = (f32[3,2,8,1024]{3,2,1,0:T(8,128)S(1)}, f32[3,2,8,1024]{3,2,1,0:T(8,128)S(1)}, u32[]{:S(2)}, u32[]{:S(2)}) collective-permute-start(f32[3,2,8,1024]{3,2,1,0:T(8,128)S(1)} %pad_maximum_fusion.refs_0_), channel_id=1, source_target_pairs={{0,1},{1,0},{2,3},{3,2},{4,5},{5,4},{6,7},{7,6},{8,9},{9,8},{10,11... | collective-permute-start | bytes 589832 | tf_op jit(solution)/shard_map/ppermute | solution.py:185
  8.9 4.5 %collective-permute-start = (f32[2,8,1024]{2,1,0:T(8,128)S(1)}, f32[2,8,1024]{2,1,0:T(8,128)S(1)}, u32[]{:S(2)}, u32[]{:S(2)}) collective-permute-start(f32[2,8,1024]{2,1,0:T(8,128)S(1)} %columns.1), channel_id=1, source_target_pairs={{0,4},{1,5},{2,6},{3,7},{4,0},{5,1},{6,2},{7,3},{8,12},{9,13},{10,... | collective-permute-start | bytes 196616 | tf_op jit(solution)/shard_map/ppermute | solution.py:185
  13.4 0.7 %copy-start.1 = (s32[2,8,1]{1,2,0:T(1,128)S(1)}, s32[2,8,1]{1,2,0:T(1,128)}, u32[]{:S(2)}) copy-start(s32[2,8,1]{1,2,0:T(1,128)} %param.7) | copy-start | bytes 196
  13.4 0.7 %copy-start = (f32[2,9]{1,0:T(2,128)S(1)}, f32[2,9]{1,0:T(2,128)}, u32[]{:S(2)}) copy-start(f32[2,9]{1,0:T(2,128)} %psf_hbm.1) | copy-start | bytes 220
  13.4 2.1 %collective-permute-start.1 = (f32[1,2,8,1024]{3,2,1,0:T(8,128)S(1)}, f32[1,2,8,1024]{3,2,1,0:T(8,128)S(1)}, u32[]{:S(2)}, u32[]{:S(2)}) collective-permute-start(f32[1,2,8,1024]{3,2,1,0:T(8,128)S(1)} %bitcast.6), channel_id=1, source_target_pairs={{0,1},{1,0},{2,3},{3,2},{4,5},{5,4},{6,7},{7,6},{8,9},{9,8},{10,11... | collective-permute-start | bytes 196616 | tf_op jit(solution)/shard_map/ppermute | solution.py:185
  15.8 6.1 %collective-permute-start.5 = (f32[2,8,1024]{2,1,0:T(8,128)S(1)}, f32[2,8,1024]{2,1,0:T(8,128)S(1)}, u32[]{:S(2)}, u32[]{:S(2)}) collective-permute-start(f32[2,8,1024]{2,1,0:T(8,128)S(1)} %get-tuple-element.17), channel_id=1, source_target_pairs={{0,8},{1,9},{2,10},{3,11},{4,12},{5,13},{6,14},{7,15},{8,16},{9,17... | collective-permute-start | bytes 196616 | tf_op jit(solution)/shard_map/ppermute | solution.py:193
  17.4 4.5 %collective-permute-start.7 = (f32[2,8,1024]{2,1,0:T(8,128)S(1)}, f32[2,8,1024]{2,1,0:T(8,128)S(1)}, u32[]{:S(2)}, u32[]{:S(2)}) collective-permute-start(f32[2,8,1024]{2,1,0:T(8,128)S(1)} %get-tuple-element.19), channel_id=1, source_target_pairs={{0,24},{1,25},{2,26},{3,27},{4,28},{5,29},{6,30},{7,31},{8,0},{9,1... | collective-permute-start | bytes 196616 | tf_op jit(solution)/shard_map/ppermute | solution.py:193
  19.5 2.5 %collective-permute-start.8 = (f32[2,8,1024]{2,1,0:T(8,128)S(1)}, f32[2,8,1024]{2,1,0:T(8,128)S(1)}, u32[]{:S(2)}, u32[]{:S(2)}) collective-permute-start(f32[2,8,1024]{2,1,0:T(8,128)S(1)} %get-tuple-element.20), channel_id=1, source_target_pairs={{0,1},{1,0},{2,3},{3,2},{4,5},{5,4},{6,7},{7,6},{8,9},{9,8},{10,11... | collective-permute-start | bytes 196616 | tf_op jit(solution)/shard_map/ppermute | solution.py:193
  19.7 6.2 %collective-permute-start.6 = (f32[2,8,1024]{2,1,0:T(8,128)S(1)}, f32[2,8,1024]{2,1,0:T(8,128)S(1)}, u32[]{:S(2)}, u32[]{:S(2)}) collective-permute-start(f32[2,8,1024]{2,1,0:T(8,128)S(1)} %get-tuple-element.18), channel_id=1, source_target_pairs={{0,16},{1,17},{2,18},{3,19},{4,20},{5,21},{6,22},{7,23},{8,24},{9,... | collective-permute-start | bytes 196616 | tf_op jit(solution)/shard_map/ppermute | solution.py:193

commit v5 on v4

--- a/solution.py
+++ b/solution.py
@@ -20,39 +20,58 @@
     return [x[:, i : i + LANES] for i in range(0, x.shape[1], LANES)]
 
 
+def moved(tiles, first, reach, lane, count):
+    if not reach:
+        return tiles[first : first + count]
+    turned = [pltpu.roll(t, (-reach) % LANES, 1) for t in tiles]
+    made = []
+    for i in range(first, first + count):
+        if reach > 0:
+            other = turned[i + 1] if i + 1 < len(turned) else jnp.zeros_like(turned[i])
+            made.append(jnp.where(lane < LANES - reach, turned[i], other))
+        else:
+            other = turned[i - 1] if i else jnp.zeros_like(turned[i])
+            made.append(jnp.where(lane >= -reach, turned[i], other))
+    return made
+
+
 def columns_kernel(science_hbm, variance_hbm, psf_hbm, out_ref, science, variance, psf, sems):
     copies = [
         pltpu.make_async_copy(source, target, sems.at[i])
         for i, (source, target) in enumerate(
-            ((variance_hbm, variance), (science_hbm, science), (psf_hbm, psf))
+            ((psf_hbm, psf), (variance_hbm, variance), (science_hbm, science))
         )
     ]
     for copy in copies:
         copy.start()
     slots, height, _ = science.shape
     taps = psf.shape[1]
-    radius = taps // 2
+    inner = 3 if taps % 6 == 3 else 1
+    outer = taps // inner
     lane = lax.broadcasted_iota(jnp.int32, (2 * height, LANES), 1)
     psi_row = lax.broadcasted_iota(jnp.int32, (2 * height, LANES), 0) < height
-    for copy in copies:
+    for copy in copies[1:]:
         copy.wait()
+    pairs = []
     for e in range(slots):
         inverse = 1.0 / variance[e]
-        pair = tiles_of(jnp.concatenate([science[e] * inverse, inverse], axis=0))
-        zero = jnp.zeros_like(pair[0])
-        summed = [zero] * len(pair)
-        for k in range(taps):
-            w = psf[e, k]
-            weight = jnp.where(psi_row, w, w * w)
-            reach = k - radius
-            moved = pair
-            if reach:
-                turned = [pltpu.roll(t, (-reach) % LANES, 1) for t in pair]
-                if reach > 0:
-                    moved = [jnp.where(lane < LANES - reach, a, b) for a, b in zip(turned, turned[1:] + [zero])]
-                else:
-                    moved = [jnp.where(lane >= -reach, a, b) for a, b in zip(turned, [zero] + turned[:-1])]
-            summed = [s + weight * m for s, m in zip(summed, moved)]
+        pairs.append(jnp.concatenate([science[e] * inverse, inverse], axis=0))
+    copies[0].wait()
+    for e, pair in enumerate(pairs):
+        zero = jnp.zeros((2 * height, LANES), jnp.float32)
+        tiles = [zero] + tiles_of(pair) + [zero]
+        count = len(tiles)
+        near = [moved(tiles, 0, i - inner // 2, lane, count) for i in range(inner)]
+        summed = None
+        for j in range(outer):
+            group = None
+            for i in range(inner):
+                w = psf[e, j * inner + i]
+                weight = jnp.where(psi_row, w, w * w)
+                terms = [weight * t for t in near[i]]
+                group = terms if group is None else [g + t for g, t in zip(group, terms)]
+            placed = moved(group, 1, (j - outer // 2) * inner, lane, count - 2)
+            summed = placed if summed is None else [s + p for s, p in zip(summed, placed)]
         out_ref[e] = jnp.concatenate(summed, axis=1)
 
 
@@ -231,7 +250,7 @@
         twin_last = send(last, "vel", sibling)
         origins = [list(range(sources))] + [[t.index(v) for v in range(sources)] for t in rounds]
         origins = origins + [[row[v ^ 1] for v in range(sources)] for row in origins]
-        groups = [[own, last], [twin], [twin_last]]
+        groups = [[own, last], [twin, twin_last]]
         depths = [sum(p.shape[0] for p in g) * slots * paired for g in groups]
         column, *parts = pl.pallas_call(
             functools.partial(matrix_kernel, steps, origins, height),
@@ -243,7 +262,7 @@
             name="matrix",
         )(psf, shifts)
         partial = []
-        for name, group, left in zip(("early", "middle", "late"), groups, parts):
+        for name, group, left in zip(("early", "late"), groups, parts):
             shapes = [jax.ShapeDtypeStruct((2 * rows_all, breadth), jnp.float32)]
             if name == "late":
                 shapes = [chunk] * order

time: 26.7 us -> 26.3 us (0.985)
  Pallas kernels: 2.72 us -> 2.41 us
    pallas_call x3 -> x2, Pallas kernels: 0.91 us -> 0.65 us  [per_device(): pl.pallas_call(functools.partial(stack_kernel, len(group), bool(partial))...]
  transfers between devices with their start and end apart: 9 -> 9, of which waited for: 4 -> 4; matrix products, arithmetic and copies ran while one was open for 0% -> 0% of each run, Pallas kernels for 5% -> 4%
where the time goes in v5:
time: 26.3 us; the launch traced here: 26.1 us
  starting transfers between devices  11.4 us (43%)
  waiting for transfers between devices  10.9 us (41%)
  Pallas kernels  2.41 us (9%)
  local copies, waits for them, and re-layouts  0.69 us (3%)
  other arithmetic  0.68 us (3%)
    ppermute x5, waiting for transfers between devices, send(): return lax.ppermute(array, axis, list(enumerate(targets)))  7.03 us
    ppermute x4, starting transfers between devices, hand(): return lax.ppermute(array, ('epoch', 'vel'), pairs)  6.13 us
    ppermute x5, starting transfers between devices, send(): return lax.ppermute(array, axis, list(enumerate(targets)))  5.26 us
    ppermute x4, waiting for transfers between devices, hand(): return lax.ppermute(array, ('epoch', 'vel'), pairs)  3.86 us
    pallas_call x1, Pallas kernels, per_device(): pl.pallas_call(columns_kernel, out_shape=jax.ShapeDtypeStruct((slots, pai...  1.02 us
    pallas_call x1, Pallas kernels, per_device(): pl.pallas_call(functools.partial(matrix_kernel, steps, origins, height),...  0.74 us
    unnamed x4, local copies, waits for them, and re-layouts  0.69 us
    pallas_call x2, Pallas kernels, per_device(): pl.pallas_call(functools.partial(stack_kernel, len(group), bool(partial))...  0.65 us
  transfers between devices with their start and end apart: 9, of which 4 were waited for; matrix products, arithmetic and copies ran while one was open for 0% of the time, Pallas kernels for 4%

profile of v5, /device:TPU:0, one launch (start us, length us, event | category | flops | bytes accessed | tf_op | source)
XLA Modules:
  0.0 26.1 jit_solution(184745840171636065)
XLA Ops:
  0.0 1.0 %columns.1 = f32[2,8,1024]{2,1,0:T(8,128)S(1)} custom-call(f32[2,4,1024]{2,1,0:T(4,128)} %science_hbm.1, f32[2,4,1024]{2,1,0:T(4,128)} %variance_hbm.1, f32[2,9]{1,0:T(2,128)} %psf_hbm.1), custom_call_target="tpu_custom_call" | custom-call | tf_op jit(solution)/shard_map/columns/pallas_call | solution.py:224
  1.0 3.0 %collective-permute-start = (f32[2,8,1024]{2,1,0:T(8,128)S(1)}, f32[2,8,1024]{2,1,0:T(8,128)S(1)}, u32[]{:S(2)}, u32[]{:S(2)}) collective-permute-start(f32[2,8,1024]{2,1,0:T(8,128)S(1)} %columns.1), channel_id=1, source_target_pairs={{0,2},{1,3},{2,4},{3,5},{4,6},{5,7},{6,0},{7,1},{8,10},{9,11},{10,... | collective-permute-start | bytes 196616 | tf_op jit(solution)/shard_map/ppermute | solution.py:204
  4.0 1.0 %collective-permute-start.1 = (f32[2,8,1024]{2,1,0:T(8,128)S(1)}, f32[2,8,1024]{2,1,0:T(8,128)S(1)}, u32[]{:S(2)}, u32[]{:S(2)}) collective-permute-start(f32[2,8,1024]{2,1,0:T(8,128)S(1)} %columns.1), channel_id=1, source_target_pairs={{0,6},{1,7},{2,0},{3,1},{4,2},{5,3},{6,4},{7,5},{8,14},{9,15},{10,... | collective-permute-start | bytes 196616 | tf_op jit(solution)/shard_map/ppermute | solution.py:204
  5.1 2.3 %collective-permute-done = f32[2,8,1024]{2,1,0:T(8,128)S(1)} collective-permute-done((f32[2,8,1024]{2,1,0:T(8,128)S(1)}, f32[2,8,1024]{2,1,0:T(8,128)S(1)}, u32[]{:S(2)}, u32[]{:S(2)}) %collective-permute-start) | collective-permute-done | bytes 65568 | tf_op jit(solution)/shard_map/ppermute | solution.py:204
  7.3 1.4 %collective-permute-done.1 = f32[2,8,1024]{2,1,0:T(8,128)S(1)} collective-permute-done((f32[2,8,1024]{2,1,0:T(8,128)S(1)}, f32[2,8,1024]{2,1,0:T(8,128)S(1)}, u32[]{:S(2)}, u32[]{:S(2)}) %collective-permute-start.1) | collective-permute-done | bytes 65568 | tf_op jit(solution)/shard_map/ppermute | solution.py:204
  8.8 0.1 collective-permute-start.2
  8.8 1.1 %collective-permute-start.3 = (f32[2,8,1024]{2,1,0:T(8,128)S(1)}, f32[2,8,1024]{2,1,0:T(8,128)S(1)}, u32[]{:S(2)}, u32[]{:S(2)}) collective-permute-start(f32[2,8,1024]{2,1,0:T(8,128)S(1)} %columns.1), channel_id=1, source_target_pairs={{0,4},{1,5},{2,6},{3,7},{4,0},{5,1},{6,2},{7,3},{8,12},{9,13},{10,... | collective-permute-start | bytes 196616 | tf_op jit(solution)/shard_map/ppermute | solution.py:204
  10.0 3.3 %collective-permute-done.3 = f32[2,8,1024]{2,1,0:T(8,128)S(1)} collective-permute-done((f32[2,8,1024]{2,1,0:T(8,128)S(1)}, f32[2,8,1024]{2,1,0:T(8,128)S(1)}, u32[]{:S(2)}, u32[]{:S(2)}) %collective-permute-start.3) | collective-permute-done | bytes 65568 | tf_op jit(solution)/shard_map/ppermute | solution.py:204
  13.3 0.0 copy-start.1
  13.3 0.0 copy-start
  13.3 0.0 collective-permute-start.4
  13.3 0.7 %copy-done.1 = s32[2,8,1]{1,2,0:T(1,128)S(1)} copy-done((s32[2,8,1]{1,2,0:T(1,128)S(1)}, s32[2,8,1]{1,2,0:T(1,128)}, u32[]{:S(2)}) %copy-start.1) | copy-done | bytes 88
  14.0 0.0 copy-done
  14.0 0.7 %matrix.1 = (s32[2,8,128]{2,1,0:T(8,128)S(1)}, bf16[64,192]{1,0:T(8,128)(2,1)S(1)}, bf16[64,192]{1,0:T(8,128)(2,1)S(1)}) custom-call(f32[2,9]{1,0:T(2,128)S(1)} %copy-done, s32[2,8]{1,0:T(2,128)S(1)} %bitcast.8), custom_call_target="tpu_custom_call" | custom-call | tf_op jit(solution)/shard_map/matrix/pallas_call | solution.py:255
  14.8 0.3 %shard_map.46.refs_2_ = f32[64,1024]{1,0:T(8,128)S(1)} custom-call(s32[2,8,128]{2,1,0:T(8,128)S(1)} %get-tuple-element.12.column_ref, bf16[64,192]{1,0:T(8,128)(2,1)S(1)} %get-tuple-element.14.parts_ref, f32[3,2,8,1024]{3,2,1,0:T(8,128)S(1)} %pad_maximum_fusion.refs_0_, f32[1,2,8,1024]{3,2,1,0:T(8,128)S(1)} %bitcast.7), custom_call_target="tpu_custom_call" | custom-call | tf_op jit(solution)/shard_map/pallas_call | solution.py:270
  15.1 0.0 collective-permute-done.4.refs_1_
  15.1 0.0 collective-permute-done.2.refs_0_
  15.1 0.3 %shard_map.47 = (f32[2,8,1024]{2,1,0:T(8,128)S(1)}, f32[2,8,1024]{2,1,0:T(8,128)S(1)}, f32[2,8,1024]{2,1,0:T(8,128)S(1)}, f32[2,8,1024]{2,1,0:T(8,128)S(1)}) custom-call(s32[2,8,128]{2,1,0:T(8,128)S(1)} %get-tuple-element.12.column_ref, bf16[64,192]{1,0:T(8,128)(2,1)S(1)} %get-tuple-element.13.parts_ref, ...), custom_call_target="tpu_custom_call" | custom-call | tf_op jit(solution)/shard_map/pallas_call | solution.py:270
  15.5 1.6 %collective-permute-start.5 = (f32[2,8,1024]{2,1,0:T(8,128)S(1)}, f32[2,8,1024]{2,1,0:T(8,128)S(1)}, u32[]{:S(2)}, u32[]{:S(2)}) collective-permute-start(f32[2,8,1024]{2,1,0:T(8,128)S(1)} %get-tuple-element.15), channel_id=1, source_target_pairs={{0,8},{1,9},{2,10},{3,11},{4,12},{5,13},{6,14},{7,15},{8,16},{9,17... | collective-permute-start | bytes 196616 | tf_op jit(solution)/shard_map/ppermute | solution.py:212
  17.1 2.1 %collective-permute-start.7 = (f32[2,8,1024]{2,1,0:T(8,128)S(1)}, f32[2,8,1024]{2,1,0:T(8,128)S(1)}, u32[]{:S(2)}, u32[]{:S(2)}) collective-permute-start(f32[2,8,1024]{2,1,0:T(8,128)S(1)} %get-tuple-element.17), channel_id=1, source_target_pairs={{0,24},{1,25},{2,26},{3,27},{4,28},{5,29},{6,30},{7,31},{8,0},{9,1... | collective-permute-start | bytes 196616 | tf_op jit(solution)/shard_map/ppermute | solution.py:212
  19.2 0.1 collective-permute-start.8
  19.3 2.2 %collective-permute-start.6 = (f32[2,8,1024]{2,1,0:T(8,128)S(1)}, f32[2,8,1024]{2,1,0:T(8,128)S(1)}, u32[]{:S(2)}, u32[]{:S(2)}) collective-permute-start(f32[2,8,1024]{2,1,0:T(8,128)S(1)} %get-tuple-element.16), channel_id=1, source_target_pairs={{0,16},{1,17},{2,18},{3,19},{4,20},{5,21},{6,22},{7,23},{8,24},{9,... | collective-permute-start | bytes 196616 | tf_op jit(solution)/shard_map/ppermute | solution.py:212
  21.6 0.0 collective-permute-done.5
  21.6 0.0 collective-permute-done.7
  21.7 0.0 collective-permute-done.8
  21.7 3.8 %collective-permute-done.6 = f32[2,8,1024]{2,1,0:T(8,128)S(1)} collective-permute-done((f32[2,8,1024]{2,1,0:T(8,128)S(1)}, f32[2,8,1024]{2,1,0:T(8,128)S(1)}, u32[]{:S(2)}, u32[]{:S(2)}) %collective-permute-start.6) | collective-permute-done | bytes 65568 | tf_op jit(solution)/shard_map/ppermute | solution.py:212
  25.5 0.6 %fusion.1 = f32[1,8,1024]{2,1,0:T(8,128)} fusion(f32[2,8,1024]{2,1,0:T(8,128)S(1)} %broadcast_select_fusion, f32[2,8,1024]{2,1,0:T(8,128)S(1)} %broadcast_select_fusion.1, f32[2,8,1024]{2,1,0:T(8,128)S(1)} %collective-permute-done.6, f32[2,8,1024]{2,1,0:T(8,128)S(1)} %broadcast_select_fusion.2), kind=kLoop, calls=%fused_computation.3 | loop fusion | flops 57344 | bytes 294912 | tf_op jit(solution)/shard_map/div | solution.py:293
  (4 shorter events, 0.0 us)
Async XLA Ops:
  1.0 6.3 %collective-permute-start = (f32[2,8,1024]{2,1,0:T(8,128)S(1)}, f32[2,8,1024]{2,1,0:T(8,128)S(1)}, u32[]{:S(2)}, u32[]{:S(2)}) collective-permute-start(f32[2,8,1024]{2,1,0:T(8,128)S(1)} %columns.1), channel_id=1, source_target_pairs={{0,2},{1,3},{2,4},{3,5},{4,6},{5,7},{6,0},{7,1},{8,10},{9,11},{10,... | collective-permute-start | bytes 196616 | tf_op jit(solution)/shard_map/ppermute | solution.py:204
  4.0 4.7 %collective-permute-start.1 = (f32[2,8,1024]{2,1,0:T(8,128)S(1)}, f32[2,8,1024]{2,1,0:T(8,128)S(1)}, u32[]{:S(2)}, u32[]{:S(2)}) collective-permute-start(f32[2,8,1024]{2,1,0:T(8,128)S(1)} %columns.1), channel_id=1, source_target_pairs={{0,6},{1,7},{2,0},{3,1},{4,2},{5,3},{6,4},{7,5},{8,14},{9,15},{10,... | collective-permute-start | bytes 196616 | tf_op jit(solution)/shard_map/ppermute | solution.py:204
  8.8 6.4 %collective-permute-start.2 = (f32[3,2,8,1024]{3,2,1,0:T(8,128)S(1)}, f32[3,2,8,1024]{3,2,1,0:T(8,128)S(1)}, u32[]{:S(2)}, u32[]{:S(2)}) collective-permute-start(f32[3,2,8,1024]{3,2,1,0:T(8,128)S(1)} %pad_maximum_fusion.refs_0_), channel_id=1, source_target_pairs={{0,1},{1,0},{2,3},{3,2},{4,5},{5,4},{6,7},{7,6},{8,9},{9,8},{10,11... | collective-permute-start | bytes 589832 | tf_op jit(solution)/shard_map/ppermute | solution.py:204
  8.8 4.5 %collective-permute-start.3 = (f32[2,8,1024]{2,1,0:T(8,128)S(1)}, f32[2,8,1024]{2,1,0:T(8,128)S(1)}, u32[]{:S(2)}, u32[]{:S(2)}) collective-permute-start(f32[2,8,1024]{2,1,0:T(8,128)S(1)} %columns.1), channel_id=1, source_target_pairs={{0,4},{1,5},{2,6},{3,7},{4,0},{5,1},{6,2},{7,3},{8,12},{9,13},{10,... | collective-permute-start | bytes 196616 | tf_op jit(solution)/shard_map/ppermute | solution.py:204
  13.3 0.7 %copy-start.1 = (s32[2,8,1]{1,2,0:T(1,128)S(1)}, s32[2,8,1]{1,2,0:T(1,128)}, u32[]{:S(2)}) copy-start(s32[2,8,1]{1,2,0:T(1,128)} %param.7) | copy-start | bytes 196
  13.3 0.7 %copy-start = (f32[2,9]{1,0:T(2,128)S(1)}, f32[2,9]{1,0:T(2,128)}, u32[]{:S(2)}) copy-start(f32[2,9]{1,0:T(2,128)} %psf_hbm.1) | copy-start | bytes 220
  13.3 1.8 %collective-permute-start.4 = (f32[1,2,8,1024]{3,2,1,0:T(8,128)S(1)}, f32[1,2,8,1024]{3,2,1,0:T(8,128)S(1)}, u32[]{:S(2)}, u32[]{:S(2)}) collective-permute-start(f32[1,2,8,1024]{3,2,1,0:T(8,128)S(1)} %bitcast.6), channel_id=1, source_target_pairs={{0,1},{1,0},{2,3},{3,2},{4,5},{5,4},{6,7},{7,6},{8,9},{9,8},{10,11... | collective-permute-start | bytes 196616 | tf_op jit(solution)/shard_map/ppermute | solution.py:204
  15.5 6.1 %collective-permute-start.5 = (f32[2,8,1024]{2,1,0:T(8,128)S(1)}, f32[2,8,1024]{2,1,0:T(8,128)S(1)}, u32[]{:S(2)}, u32[]{:S(2)}) collective-permute-start(f32[2,8,1024]{2,1,0:T(8,128)S(1)} %get-tuple-element.15), channel_id=1, source_target_pairs={{0,8},{1,9},{2,10},{3,11},{4,12},{5,13},{6,14},{7,15},{8,16},{9,17... | collective-permute-start | bytes 196616 | tf_op jit(solution)/shard_map/ppermute | solution.py:212
  17.1 4.5 %collective-permute-start.7 = (f32[2,8,1024]{2,1,0:T(8,128)S(1)}, f32[2,8,1024]{2,1,0:T(8,128)S(1)}, u32[]{:S(2)}, u32[]{:S(2)}) collective-permute-start(f32[2,8,1024]{2,1,0:T(8,128)S(1)} %get-tuple-element.17), channel_id=1, source_target_pairs={{0,24},{1,25},{2,26},{3,27},{4,28},{5,29},{6,30},{7,31},{8,0},{9,1... | collective-permute-start | bytes 196616 | tf_op jit(solution)/shard_map/ppermute | solution.py:212
  19.2 2.5 %collective-permute-start.8 = (f32[2,8,1024]{2,1,0:T(8,128)S(1)}, f32[2,8,1024]{2,1,0:T(8,128)S(1)}, u32[]{:S(2)}, u32[]{:S(2)}) collective-permute-start(f32[2,8,1024]{2,1,0:T(8,128)S(1)} %get-tuple-element.18), channel_id=1, source_target_pairs={{0,1},{1,0},{2,3},{3,2},{4,5},{5,4},{6,7},{7,6},{8,9},{9,8},{10,11... | collective-permute-start | bytes 196616 | tf_op jit(solution)/shard_map/ppermute | solution.py:212
  19.3 6.2 %collective-permute-start.6 = (f32[2,8,1024]{2,1,0:T(8,128)S(1)}, f32[2,8,1024]{2,1,0:T(8,128)S(1)}, u32[]{:S(2)}, u32[]{:S(2)}) collective-permute-start(f32[2,8,1024]{2,1,0:T(8,128)S(1)} %get-tuple-element.16), channel_id=1, source_target_pairs={{0,16},{1,17},{2,18},{3,19},{4,20},{5,21},{6,22},{7,23},{8,24},{9,... | collective-permute-start | bytes 196616 | tf_op jit(solution)/shard_map/ppermute | solution.py:212
